TPU v7x, 32 devices: a whole 2x2x4 slice. The times are simulated.
32 devices in a mesh: rows: 8 (over z, y), cols: 4 (over x, core).
Axes of the slice: x: 2, y: 2, z: 4, core: 2. Of those that a mesh axis runs over, the one named last changes fastest.
Arguments:
- hblocks: float32 [64, 24, 128, 128], P('rows'), may hold values from -0.0546875 to 0.0546875
- col_index: int32 [64, 24], P('rows'), may hold values from 0 to 63, as said below
- right_side: float32 [64, 64, 128], P('rows', 'cols'), may hold values from -12 to 12
- center: float32 [1], replicated, may hold values from -0.5 to 0.5
- shifts: float32 [8], replicated, may hold values from 0.05 to 2
- filter_weights: float32 [8], replicated, may hold values from 0.03 to 0.3
Outputs:
- filtered: float32 [64, 64, 128], P('rows', 'cols')
- gram_matrix: float32 [64, 64], P(None, 'cols')
- ritz_matrix: float32 [64, 64], P(None, 'cols')
Inputs may be any that keep to these rules, and one draw needn't show every extreme that they name: `col_index`: block rows are held 8 to a device of rows, in order. In block row i the first 8 column indices are the 8 block rows of the device that holds i, each once. Every other column index of a block row lies on another device of rows; for each pair of distinct devices, the block rows of the one that are named by the block rows of the other are exactly 2 distinct ones.
All inputs are finite; a program needn't handle non-finite values.
Results may differ from a plain program's by a relative error of at most 0.0001.
Values sent between devices are 32-bit elements; how exact they have to be, the bound alone decides.
A program may use at most 64 MiB of HBM per device.

v0:
```python
import functools

import jax
import jax.numpy as jnp
from jax import lax
from jax.experimental import pallas as pl
from jax.experimental.pallas import tpu as pltpu
from jax.sharding import PartitionSpec as P

CAP = 2


exact_mode = lax.Precision.HIGHEST


def column_dot(first_arr, second_arr):
    return jnp.sum(first_arr * second_arr, axis=(0, 2))


def ordered_lists(need_mask, slot_width):
    ranks = jnp.cumsum(need_mask, axis=1)
    positions = lax.broadcasted_iota(jnp.int32, need_mask.shape, 1)
    columns_out = []
    for slot in range(slot_width):
        hit = (need_mask > 0) & (ranks == slot + 1)
        columns_out.append(jnp.sum(jnp.where(hit, positions, 0), axis=1))
    lists = jnp.stack(columns_out, axis=1)
    live = jnp.sum(need_mask, axis=1, keepdims=True) > 0
    return jnp.where(live, lists, -1)


def filter_factors(alpha_one, beta_one, alpha_two, delta_shift, weights):
    zeta_one = 1.0 / (1.0 + delta_shift * alpha_one)
    zeta_two = (
        zeta_one
        * alpha_one
        / (alpha_two * beta_one * (1.0 - zeta_one) + alpha_one * (1.0 + delta_shift * alpha_two))
    )
    from_start = jnp.sum(
        weights * (alpha_one * zeta_one + alpha_two * beta_one * zeta_one * zeta_two), axis=0
    )
    from_residual = jnp.sum(weights * (alpha_two * zeta_two), axis=0)
    return from_start, from_residual


def shards(hblocks, col_index, right_side, center, shifts, filter_weights):
    block_rows = hblocks.shape[0]
    block_width = hblocks.shape[2]
    local_vecs = right_side.shape[1]
    pole_count = shifts.shape[0]
    peer_count = lax.axis_size("rows")
    slot_width = CAP
    device_index = lax.axis_index("rows")
    own_cols = col_index[:, :block_rows] - device_index * block_rows
    far_cols = col_index[:, block_rows:].reshape(-1)
    near_blocks = hblocks[:, :block_rows]
    far_blocks = hblocks[:, block_rows:]
    every_key = jnp.arange(peer_count * block_rows, dtype=jnp.int32)
    need_mask = (
        jnp.any(far_cols[:, None] == every_key[None, :], axis=0)
        .astype(jnp.int32)
        .reshape(peer_count, block_rows)
    )
    incoming_mask = lax.all_to_all(need_mask, "rows", split_axis=0, concat_axis=0, tiled=True)
    send_lists = ordered_lists(incoming_mask, slot_width)
    my_lists = ordered_lists(need_mask, slot_width)
    owners = lax.broadcasted_iota(jnp.int32, my_lists.shape, 0)
    slot_keys = jnp.where(my_lists >= 0, owners * block_rows + my_lists, -1).reshape(-1)
    slot_total = slot_keys.shape[0]
    matches = far_cols[:, None] == slot_keys[None, :]
    picker = matches.astype(jnp.float32)
    slot_numbers = lax.broadcasted_iota(jnp.int32, matches.shape, 1)
    slot_of_ref = jnp.sum(jnp.where(matches, slot_numbers, 0), axis=1)
    row_numbers = jnp.arange(block_rows, dtype=jnp.int32)[:, None]
    spread = (send_lists.reshape(-1)[None, :] == row_numbers).astype(jnp.float32)
    own_spread = (own_cols.reshape(-1)[None, :] == row_numbers).astype(jnp.float32)
    send_index = jnp.maximum(send_lists, 0)
    send_live = (send_lists >= 0)[:, :, None, None]

    def apply_h(vector):
        far_terms = jnp.einsum("ikab,iva->ikvb", far_blocks, vector, precision=exact_mode).reshape(
            far_cols.shape[0], -1
        )
        slot_sums = jnp.dot(picker.T, far_terms, precision=exact_mode).reshape(
            peer_count, slot_width, local_vecs, block_width
        )
        picked = vector[send_index]
        outgoing = jnp.where(send_live, picked, jnp.zeros_like(picked))
        both = lax.all_to_all(
            jnp.concatenate([outgoing, slot_sums], axis=1),
            "rows",
            split_axis=0,
            concat_axis=0,
            tiled=True,
        )
        arrived = both[:, :slot_width].reshape(slot_total, local_vecs, block_width)
        returned = both[:, slot_width:].reshape(slot_total, -1)
        near_vec = vector[own_cols]
        result = jnp.einsum("ikab,ikvb->iva", near_blocks, near_vec, precision=exact_mode)
        near_terms = jnp.einsum(
            "ikab,iva->ikvb", near_blocks, vector, precision=exact_mode
        ).reshape(block_rows * block_rows, -1)
        result = result + jnp.dot(own_spread, near_terms, precision=exact_mode).reshape(
            vector.shape
        )
        far_vec = arrived[slot_of_ref]
        far_vec = far_vec.reshape(block_rows, -1, local_vecs, block_width)
        result = result + jnp.einsum("ikab,ikvb->iva", far_blocks, far_vec, precision=exact_mode)
        return result + jnp.dot(spread, returned, precision=exact_mode).reshape(vector.shape)

    def wide(per_column):
        return per_column[None, :, None]

    center_value = center[0]
    base_shift = jnp.min(shifts)
    delta_shift = (shifts - base_shift)[:, None]
    start = right_side
    start_image = apply_h(start)
    half_one = start_image - center_value * start
    start_norm, half_norm = lax.psum(
        jnp.stack([column_dot(start, start), column_dot(half_one, half_one)]), "rows"
    )
    alpha_one = start_norm / (half_norm + base_shift * start_norm)
    op_image = apply_h(half_one) - center_value * half_one + base_shift * start
    residual = start - wide(alpha_one) * op_image
    residual_image = apply_h(residual)
    res_norm = lax.psum(column_dot(residual, residual), "rows")
    beta_one = res_norm / start_norm
    direction = residual + wide(beta_one) * start
    half_two = residual_image - center_value * residual + wide(beta_one) * half_one
    energy = lax.psum(
        column_dot(half_two, half_two) + base_shift * column_dot(direction, direction), "rows"
    )
    from_start, from_residual = filter_factors(
        alpha_one, beta_one, res_norm / energy, delta_shift, filter_weights[:, None]
    )
    filtered = wide(from_start) * start + wide(from_residual) * residual
    applied = wide(from_start) * start_image + wide(from_residual) * residual_image
    column_piece = lax.all_gather(filtered, "cols", axis=1, tiled=True)
    correlation = jnp.einsum("iae,ibe->ab", column_piece, filtered, precision=exact_mode)
    projected = jnp.einsum("iae,ibe->ab", column_piece, applied, precision=exact_mode)
    partial_gram = jnp.stack([correlation, projected])
    summed = lax.psum(partial_gram, "rows")
    row_total = peer_count * block_rows * block_width
    return (filtered, summed[0] / row_total, summed[1] / row_total)


def split(value):
    high = value.astype(jnp.bfloat16)
    low = (value - high.astype(jnp.float32)).astype(jnp.bfloat16)
    return high, low


def pack_kernel(
    n_rows,
    me_ref,
    cols_ref,
    blocks_hbm,
    high_ref,
    low_ref,
    lists_ref,
    blocks,
    acc,
    index,
    scalars,
    sem,
    load_sems,
):
    width = blocks.shape[-1]
    block_rows, per_row = cols_ref.shape
    me = me_ref[0]

    def load(row):
        return pltpu.make_async_copy(blocks_hbm.at[row], blocks.at[row], load_sems.at[row])

    for row in range(block_rows):
        load(row).start()

    def place_blocks():
        columns = cols_ref[...].astype(jnp.float32)
        place = lax.broadcasted_iota(jnp.int32, columns.shape, 1)
        spots = columns - (me * block_rows).astype(jnp.float32)
        for step in range(1, n_rows):
            first = (lax.rem(me + step, n_rows) * block_rows).astype(jnp.float32)
            inner = columns - first
            hit = (place >= block_rows) & (inner >= 0.0) & (inner < block_rows)
            low_row = jnp.where(hit, inner, float(block_rows))
            low_row = jnp.min(jnp.min(low_row, axis=1, keepdims=True), axis=0, keepdims=True)
            high_row = jnp.where(hit, inner, -1.0)
            high_row = jnp.max(jnp.max(high_row, axis=1, keepdims=True), axis=0, keepdims=True)
            slot = float(block_rows + CAP * (step - 1)) + jnp.where(inner == high_row, 1.0, 0.0)
            spots = jnp.where(hit, slot, spots)
            lists_ref[step - 1, 0:1, :] = jnp.broadcast_to(low_row, (1, width))
            lists_ref[step - 1, 1:2, :] = jnp.broadcast_to(high_row, (1, width))
        index[...] = jnp.zeros_like(index)
        index[:, :per_row] = spots.astype(jnp.int32)
        move = pltpu.make_async_copy(index, scalars, sem)
        move.start()
        move.wait()

    place_blocks()

    @pl.loop(0, block_rows)
    def _(row):
        acc[...] = jnp.zeros_like(acc)
        load(row).wait()
        for k in range(per_row):
            spot = scalars[row, k]
            acc[spot] = acc[spot] + blocks[row, k]
        lines = pl.ds(pl.multiple_of(row * width, width), width)
        for spot in range(acc.shape[0]):
            high, low = split(acc[spot])
            high_ref[lines, spot * width : (spot + 1) * width] = high
            low_ref[lines, spot * width : (spot + 1) * width] = low


def pack_blocks(n_rows, me, col_index, hblocks, spots):
    block_rows, per_row, width, _ = hblocks.shape
    out = jax.ShapeDtypeStruct((block_rows * width, spots * width), jnp.bfloat16)
    lists = (n_rows - 1, CAP, width)
    vmem = pl.BlockSpec(memory_space=pltpu.VMEM)
    return pl.pallas_call(
        functools.partial(pack_kernel, n_rows),
        in_specs=[
            pl.BlockSpec(memory_space=pltpu.SMEM),
            vmem,
            pl.BlockSpec(memory_space=pltpu.HBM),
        ],
        out_specs=[vmem, vmem, vmem],
        scratch_shapes=[
            pltpu.VMEM(hblocks.shape, jnp.float32),
            pltpu.VMEM((spots, width, width), jnp.float32),
            pltpu.VMEM((block_rows, 128), jnp.int32),
            pltpu.SMEM((block_rows, 128), jnp.int32),
            pltpu.SemaphoreType.DMA,
            pltpu.SemaphoreType.DMA((block_rows,)),
        ],
        out_shape=[out, out, jax.ShapeDtypeStruct(lists, jnp.float32)],
        compiler_params=pltpu.CompilerParams(vmem_limit_bytes=36 << 20),
    )(me, col_index, hblocks)


def filter_kernel(
    n_rows,
    n_cols,
    center_ref,
    shifts_ref,
    weights_ref,
    vec_ref,
    lists_ref,
    high,
    low,
    out_ref,
    gram_ref,
    ritz_ref,
    lists,
    vec_send,
    vec_recv,
    prod_send,
    prod_recv,
    col_start,
    col_res,
    res_send,
    sums_send,
    sums_recv,
    factor_send,
    factors,
    gram_send,
    gram_recv,
    list_sems,
    vec_sems,
    prod_sems,
    col_sems,
    sums_sems,
    gram_sems,
):
    block_rows, vecs, width = vec_ref.shape
    mine = block_rows * width
    pair = CAP * width
    peers = n_rows - 1
    me = lax.axis_index("rows")
    me_col = lax.axis_index("cols")
    pending = []

    barrier = pltpu.get_barrier_semaphore()
    for step in range(1, n_rows):
        pl.semaphore_signal(barrier, inc=1, device_id={"rows": lax.rem(me + step, n_rows)})
    for step in range(1, n_cols):
        pl.semaphore_signal(barrier, inc=1, device_id={"cols": lax.rem(me_col + step, n_cols)})
    pl.semaphore_wait(barrier, peers + n_cols - 1)

    def to_row(src, dst, sems, step):
        copy = pltpu.make_async_remote_copy(
            src_ref=src,
            dst_ref=dst,
            send_sem=sems.at[0, step - 1],
            recv_sem=sems.at[1, peers - step],
            device_id={"rows": lax.rem(me + step, n_rows)},
            device_id_type=pl.DeviceIdType.MESH,
        )
        copy.start()
        pending.append(copy)
        return copy

    def to_col(src, dst, sems, step):
        copy = pltpu.make_async_remote_copy(
            src_ref=src,
            dst_ref=dst,
            send_sem=sems.at[0, step - 1],
            recv_sem=sems.at[1, n_cols - 1 - step],
            device_id={"cols": lax.rem(me_col + step, n_cols)},
            device_id_type=pl.DeviceIdType.MESH,
        )
        copy.start()
        pending.append(copy)
        return copy

    def arrive(copies):
        for copy in copies:
            copy.wait_recv()

    list_copies = [
        to_row(lists_ref.at[step - 1], lists.at[peers - step], list_sems, step)
        for step in range(1, n_rows)
    ]

    def flat(ref):
        return jnp.concatenate([ref[i] for i in range(block_rows)], axis=1)

    start = flat(vec_ref)

    def named(step, slot, row):
        return jnp.broadcast_to(lists[step - 1, slot : slot + 1, :], (vecs, width)) == float(row)

    def dot(a, b, transposed):
        return lax.dot_general(
            a, b, (((1,), (1 if transposed else 0,)), ((), ())),
            preferred_element_type=jnp.float32,
        )

    def times(both, top, columns, transposed):
        wide_part = dot(both, high[:, columns], transposed)
        count = top.shape[0]
        return wide_part[:count] + wide_part[count:] + dot(top, low[:, columns], transposed)

    groups = vecs // 8
    lane = lax.broadcasted_iota(jnp.int32, (8, width), 1)

    def send_sums(turn, values):
        packed = jnp.zeros((8, width), jnp.float32)
        for q, value in enumerate(values):
            for g in range(groups):
                packed = jnp.where(lane == q * groups + g, value[g * 8 : (g + 1) * 8], packed)
        sums_send[turn] = packed
        return [
            to_row(
                sums_send.at[turn],
                sums_recv.at[turn, peers - step],
                sums_sems.at[turn],
                step,
            )
            for step in range(1, n_rows)
        ]

    def total_sums(turn, copies, count):
        arrive(copies)
        total = sums_send[turn]
        for step in range(1, n_rows):
            total = total + sums_recv[turn, step - 1]
        return [
            jnp.concatenate(
                [total[:, q * groups + g : q * groups + g + 1] for g in range(groups)], axis=0
            )
            for q in range(count)
        ]

    def send_vectors(turn, vector):
        copies = []
        for step in range(1, n_rows):
            for slot in range(CAP):
                picked = jnp.zeros((vecs, width), jnp.float32)
                for row in range(block_rows):
                    piece = vector[:, row * width : (row + 1) * width]
                    picked = jnp.where(named(step, slot, row), piece, picked)
                vec_send[turn, step - 1, :, slot * width : (slot + 1) * width] = picked
            copies.append(
                to_row(
                    vec_send.at[turn, step - 1],
                    vec_recv.at[turn, peers - step],
                    vec_sems.at[turn],
                    step,
                )
            )
        return copies

    def apply_h(turn, vector, sums, later):
        if turn > 0:
            copies = send_vectors(turn, vector)
            sum_copies = send_sums(turn - 1, sums)
        top, bottom = split(vector)
        both = jnp.concatenate([top, bottom], axis=0)
        products = []
        for step in range(1, n_rows):
            columns = slice(mine + (step - 1) * pair, mine + step * pair)
            prod_send[turn, step - 1] = times(both, top, columns, False)
            products.append(
                to_row(
                    prod_send.at[turn, step - 1],
                    prod_recv.at[turn, peers - step],
                    prod_sems.at[turn],
                    step,
                )
            )
        if turn == 0:
            arrive(list_copies)
            copies = send_vectors(turn, vector)
            sum_copies = None
        if later is not None:
            col_copies.extend(later())
        near = slice(0, mine)
        result = times(both, top, near, False) + times(both, top, near, True)
        for step in range(1, n_rows):
            copies[peers - step].wait_recv()
            top, bottom = split(vec_recv[turn, step - 1])
            both = jnp.concatenate([top, bottom], axis=0)
            columns = slice(mine + (step - 1) * pair, mine + step * pair)
            result = result + times(both, top, columns, True)
        pieces = [result[:, row * width : (row + 1) * width] for row in range(block_rows)]
        for step in range(1, n_rows):
            products[peers - step].wait_recv()
            for slot in range(CAP):
                back = prod_recv[turn, step - 1, :, slot * width : (slot + 1) * width]
                for row in range(block_rows):
                    pieces[row] = pieces[row] + jnp.where(named(step, slot, row), back, 0.0)
        return jnp.concatenate(pieces, axis=1), sum_copies

    def column_sum(value):
        return jnp.sum(value, axis=1, keepdims=True)

    center = center_ref[0]
    poles = [shifts_ref[m] for m in range(shifts_ref.shape[0])]
    base = functools.reduce(jnp.minimum, poles)
    all_lanes = jnp.zeros((vecs, width), jnp.float32)

    col_copies = []

    def send_start():
        col_start[me_col] = vec_ref[...]
        return [
            to_col(vec_ref, col_start.at[me_col], col_sems.at[0], step)
            for step in range(1, n_cols)
        ]

    def send_residual():
        for row in range(block_rows):
            res_send[row] = residual[:, row * width : (row + 1) * width]
        col_res[me_col] = res_send[...]
        return [
            to_col(res_send, col_res.at[me_col], col_sems.at[1], step)
            for step in range(1, n_cols)
        ]

    start_image, _ = apply_h(0, start, None, send_start)
    half_one = start_image - center * start
    own_sums = [column_sum(start * start), column_sum(half_one * half_one)]
    second, sum_copies = apply_h(1, half_one, own_sums, None)
    start_norm, half_norm = total_sums(0, sum_copies, 2)
    alpha_one = start_norm / (half_norm + base * start_norm)
    op_image = second - center * half_one + base * start
    residual = start - alpha_one * op_image
    own_norm = column_sum(residual * residual)
    residual_image, sum_copies = apply_h(2, residual, [own_norm], send_residual)
    (res_norm,) = total_sums(1, sum_copies, 1)
    beta = res_norm / start_norm
    direction = residual + beta * start
    half_two = residual_image - center * residual + beta * half_one
    own_energy = column_sum(half_two * half_two + base * (direction * direction))
    (energy,) = total_sums(2, send_sums(2, [own_energy]), 1)
    alpha_one = alpha_one + all_lanes
    beta = beta + all_lanes
    alpha_two = res_norm / energy + all_lanes
    from_start = all_lanes
    from_residual = all_lanes
    for m, pole in enumerate(poles):
        delta = pole - base
        zeta_one = 1.0 / (1.0 + delta * alpha_one)
        zeta_two = (
            zeta_one
            * alpha_one
            / (
                alpha_two * beta * (1.0 - zeta_one)
                + alpha_one * (1.0 + delta * alpha_two)
            )
        )
        weight = weights_ref[m]
        from_start = from_start + weight * (
            alpha_one * zeta_one + alpha_two * beta * zeta_one * zeta_two
        )
        from_residual = from_residual + weight * (alpha_two * zeta_two)
    wide_lane = lax.broadcasted_iota(jnp.int32, (vecs, width), 1)
    factor_send[...] = jnp.where(wide_lane == 0, from_start, from_residual)
    factors[me_col] = factor_send[...]
    col_copies += [
        to_col(factor_send, factors.at[me_col], col_sems.at[2], step)
        for step in range(1, n_cols)
    ]
    along_start, along_res = from_start[:, 0:1], from_residual[:, 0:1]
    filtered = along_start * start + along_res * residual
    applied = along_start * start_image + along_res * residual_image
    for row in range(block_rows):
        out_ref[row] = filtered[:, row * width : (row + 1) * width]
    own = jnp.concatenate([filtered, applied], axis=0)
    arrive(col_copies)
    every = jnp.concatenate(
        [
            factors[c, :, 0:1] * flat(col_start.at[c]) + factors[c, :, 1:2] * flat(col_res.at[c])
            for c in range(n_cols)
        ],
        axis=0,
    )
    top, bottom = split(own)
    every_top, every_bottom = split(every)
    both = dot(jnp.concatenate([top, bottom], axis=0), every_top, True)
    count = 2 * vecs
    partial = both[:count] + both[count:] + dot(top, every_bottom, True)
    gram_send[...] = jnp.concatenate([partial[:vecs], partial[vecs:]], axis=1)
    gram_recv[me] = gram_send[...]
    gram_copies = [
        to_row(gram_send, gram_recv.at[me], gram_sems, step) for step in range(1, n_rows)
    ]
    arrive(gram_copies)
    summed = gram_recv[0]
    for device in range(1, n_rows):
        summed = summed + gram_recv[device]
    scaled = summed * (1.0 / (n_rows * mine))
    columns = n_cols * vecs
    gram_ref[...] = scaled[:, :columns]
    ritz_ref[...] = scaled[:, columns:]
    for copy in pending:
        copy.wait_send()


def fused_shards(
    n_rows, n_cols, hblocks, col_index, right_side, center, shifts, filter_weights
):
    block_rows, _, width, _ = hblocks.shape
    vecs = right_side.shape[1]
    peers = n_rows - 1
    spots = block_rows + CAP * peers
    mine = block_rows * width
    me = lax.axis_index("rows")
    high, low, lists = pack_blocks(n_rows, me.reshape(1), col_index, hblocks, spots)
    columns = n_cols * vecs
    pair = CAP * width
    vmem = pl.BlockSpec(memory_space=pltpu.VMEM)
    smem = pl.BlockSpec(memory_space=pltpu.SMEM)
    f32 = jnp.float32
    filtered, gram, ritz = pl.pallas_call(
        functools.partial(filter_kernel, n_rows, n_cols),
        out_shape=[
            jax.ShapeDtypeStruct(right_side.shape, f32),
            jax.ShapeDtypeStruct((vecs, columns), f32),
            jax.ShapeDtypeStruct((vecs, columns), f32),
        ],
        in_specs=[smem, smem, smem, vmem, vmem, vmem, vmem],
        out_specs=[vmem, vmem, vmem],
        scratch_shapes=[
            pltpu.VMEM((peers, CAP, width), f32),
            pltpu.VMEM((3, peers, vecs, pair), f32),
            pltpu.VMEM((3, peers, vecs, pair), f32),
            pltpu.VMEM((3, peers, vecs, pair), f32),
            pltpu.VMEM((3, peers, vecs, pair), f32),
            pltpu.VMEM((n_cols,) + right_side.shape, f32),
            pltpu.VMEM((n_cols,) + right_side.shape, f32),
            pltpu.VMEM(right_side.shape, f32),
            pltpu.VMEM((3, 8, width), f32),
            pltpu.VMEM((3, peers, 8, width), f32),
            pltpu.VMEM((vecs, width), f32),
            pltpu.VMEM((n_cols, vecs, width), f32),
            pltpu.VMEM((vecs, 2 * columns), f32),
            pltpu.VMEM((n_rows, vecs, 2 * columns), f32),
            pltpu.SemaphoreType.DMA((2, peers)),
            pltpu.SemaphoreType.DMA((3, 2, peers)),
            pltpu.SemaphoreType.DMA((3, 2, peers)),
            pltpu.SemaphoreType.DMA((3, 2, n_cols - 1)),
            pltpu.SemaphoreType.DMA((3, 2, peers)),
            pltpu.SemaphoreType.DMA((2, peers)),
        ],
        compiler_params=pltpu.CompilerParams(
            collective_id=0, has_side_effects=True, vmem_limit_bytes=24 << 20
        ),
    )(center, shifts, filter_weights, right_side, lists, high, low)
    return filtered, gram.T, ritz.T


def solution(mesh):
    placed = (P("rows", None, None, None), P("rows", None), P("rows", "cols", None), P(), P(), P())
    n_rows, n_cols = mesh.shape["rows"], mesh.shape["cols"]

    def body(hblocks, *rest):
        block_rows, per_row = hblocks.shape[:2]
        if CAP * (n_rows - 1) * block_rows <= block_rows * per_row:
            return fused_shards(n_rows, n_cols, hblocks, *rest)
        return shards(hblocks, *rest)

    return jax.shard_map(
        body,
        mesh=mesh,
        in_specs=placed,
        out_specs=(P("rows", "cols", None), P(None, "cols"), P(None, "cols")),
        check_vma=False,
    )
```

profile of v0, /device:TPU:0, one launch (start us, length us, event | category | flops | bytes accessed | tf_op | source)
XLA Modules:
  0.0 60.2 jit_solution(5212239336623262396)
XLA Ops:
  1.3 0.0 copy-start.1
  1.3 0.7 %copy-done.1 = s32[8,24]{1,0:T(8,128)S(1)} copy-done((s32[8,24]{1,0:T(8,128)S(1)}, s32[8,24]{1,0:T(8,128)}, u32[]{:S(2)}) %copy-start.1) | copy-done | bytes 792
  2.0 0.0 copy-start
  2.0 0.0 copy-start.2
  2.0 0.0 copy-start.3
  2.0 5.5 %shard_map.85 = (bf16[1024,2816]{1,0:T(8,128)(2,1)S(1)}, bf16[1024,2816]{1,0:T(8,128)(2,1)S(1)}, f32[7,2,128]{2,1,0:T(2,128)S(1)}) custom-call(s32[1]{0:T(128)} %bitcast.me_ref, s32[8,24]{1,0:T(8,128)S(1)} %copy-done.1, f32[8,24,128,128]{3,2,1,0:T(8,128)} %blocks_hbm.1), custom_call_target="tpu_custom_call" | custom-call | tf_op jit(solution)/shard_map/pallas_call | solution.py:222
  7.5 0.0 copy-done
  7.5 0.0 copy-done.2
  7.5 0.0 copy-done.3
  7.5 50.8 %shard_map.86 = (f32[8,16,128]{2,1,0:T(8,128)S(1)}, f32[16,64]{1,0:T(8,128)S(1)}, f32[16,64]{1,0:T(8,128)S(1)}) custom-call(f32[1]{0:T(128)S(6)} %copy.12.center_ref, f32[8]{0:T(128)S(1)} %copy-done.2, f32[8]{0:T(128)S(1)} %copy-done.3, f32[8,16,128]{2,1,0:T(8,128)S(1)} %copy-done, f32[7,2,128]{2,1,0:T(2,128)S(1)} %get-tuple-element.9.lists_ref, ...), custom_call_target="tpu_custom_call" | custom-call | tf_op jit(solution)/shard_map/pallas_call | solution.py:558
  58.3 0.6 %copy.13 = f32[8,16,128]{2,1,0:T(8,128)} copy(f32[8,16,128]{2,1,0:T(8,128)S(1)} %get-tuple-element.18) | data formatting | bytes 131072
  59.0 0.6 copy.14
  59.6 0.6 copy.15
Async XLA Ops:
  1.3 0.7 %copy-start.1 = (s32[8,24]{1,0:T(8,128)S(1)}, s32[8,24]{1,0:T(8,128)}, u32[]{:S(2)}) copy-start(s32[8,24]{1,0:T(8,128)} %cols_ref.1) | copy-start | bytes 2308
  2.0 5.5 %copy-start = (f32[8,16,128]{2,1,0:T(8,128)S(1)}, f32[8,16,128]{2,1,0:T(8,128)}, u32[]{:S(2)}) copy-start(f32[8,16,128]{2,1,0:T(8,128)} %vec_ref.1) | copy-start | bytes 196612
  2.0 5.5 %copy-start.2 = (f32[8]{0:T(128)S(1)}, f32[8]{0:T(128)}, u32[]{:S(2)}) copy-start(f32[8]{0:T(128)} %shifts_ref.1) | copy-start | bytes 100
  2.0 5.5 %copy-start.3 = (f32[8]{0:T(128)S(1)}, f32[8]{0:T(128)}, u32[]{:S(2)}) copy-start(f32[8]{0:T(128)} %weights_ref.1) | copy-start | bytes 100
where the time goes:
time: 60.3 us; the launch traced here: 60.2 us
  Pallas kernels  56.3 us (93%)
  local copies, waits for them, and re-layouts  2.52 us (4%)
  between operations  1.33 us (2%)
    pallas_call x1, Pallas kernels, fused_shards(): pl.pallas_call(functools.partial(filter_kernel, n_rows, n_cols), out_shap...  50.8 us
    pallas_call x1, Pallas kernels, pack_blocks(): pl.pallas_call(functools.partial(pack_kernel, n_rows), in_specs=[pl.Block...  5.51 us
    unnamed x11, local copies, waits for them, and re-layouts  2.52 us

commit v1 on v0

v1 whole, which is shorter than its diff:
```python
import functools

import jax
import jax.numpy as jnp
from jax import lax
from jax.experimental import pallas as pl
from jax.experimental.pallas import tpu as pltpu
from jax.sharding import PartitionSpec as P

CAP = 2


exact_mode = lax.Precision.HIGHEST


def column_dot(first_arr, second_arr):
    return jnp.sum(first_arr * second_arr, axis=(0, 2))


def ordered_lists(need_mask, slot_width):
    ranks = jnp.cumsum(need_mask, axis=1)
    positions = lax.broadcasted_iota(jnp.int32, need_mask.shape, 1)
    columns_out = []
    for slot in range(slot_width):
        hit = (need_mask > 0) & (ranks == slot + 1)
        columns_out.append(jnp.sum(jnp.where(hit, positions, 0), axis=1))
    lists = jnp.stack(columns_out, axis=1)
    live = jnp.sum(need_mask, axis=1, keepdims=True) > 0
    return jnp.where(live, lists, -1)


def filter_factors(alpha_one, beta_one, alpha_two, delta_shift, weights):
    zeta_one = 1.0 / (1.0 + delta_shift * alpha_one)
    zeta_two = (
        zeta_one
        * alpha_one
        / (alpha_two * beta_one * (1.0 - zeta_one) + alpha_one * (1.0 + delta_shift * alpha_two))
    )
    from_start = jnp.sum(
        weights * (alpha_one * zeta_one + alpha_two * beta_one * zeta_one * zeta_two), axis=0
    )
    from_residual = jnp.sum(weights * (alpha_two * zeta_two), axis=0)
    return from_start, from_residual


def shards(hblocks, col_index, right_side, center, shifts, filter_weights):
    block_rows = hblocks.shape[0]
    block_width = hblocks.shape[2]
    local_vecs = right_side.shape[1]
    pole_count = shifts.shape[0]
    peer_count = lax.axis_size("rows")
    slot_width = CAP
    device_index = lax.axis_index("rows")
    own_cols = col_index[:, :block_rows] - device_index * block_rows
    far_cols = col_index[:, block_rows:].reshape(-1)
    near_blocks = hblocks[:, :block_rows]
    far_blocks = hblocks[:, block_rows:]
    every_key = jnp.arange(peer_count * block_rows, dtype=jnp.int32)
    need_mask = (
        jnp.any(far_cols[:, None] == every_key[None, :], axis=0)
        .astype(jnp.int32)
        .reshape(peer_count, block_rows)
    )
    incoming_mask = lax.all_to_all(need_mask, "rows", split_axis=0, concat_axis=0, tiled=True)
    send_lists = ordered_lists(incoming_mask, slot_width)
    my_lists = ordered_lists(need_mask, slot_width)
    owners = lax.broadcasted_iota(jnp.int32, my_lists.shape, 0)
    slot_keys = jnp.where(my_lists >= 0, owners * block_rows + my_lists, -1).reshape(-1)
    slot_total = slot_keys.shape[0]
    matches = far_cols[:, None] == slot_keys[None, :]
    picker = matches.astype(jnp.float32)
    slot_numbers = lax.broadcasted_iota(jnp.int32, matches.shape, 1)
    slot_of_ref = jnp.sum(jnp.where(matches, slot_numbers, 0), axis=1)
    row_numbers = jnp.arange(block_rows, dtype=jnp.int32)[:, None]
    spread = (send_lists.reshape(-1)[None, :] == row_numbers).astype(jnp.float32)
    own_spread = (own_cols.reshape(-1)[None, :] == row_numbers).astype(jnp.float32)
    send_index = jnp.maximum(send_lists, 0)
    send_live = (send_lists >= 0)[:, :, None, None]

    def apply_h(vector):
        far_terms = jnp.einsum("ikab,iva->ikvb", far_blocks, vector, precision=exact_mode).reshape(
            far_cols.shape[0], -1
        )
        slot_sums = jnp.dot(picker.T, far_terms, precision=exact_mode).reshape(
            peer_count, slot_width, local_vecs, block_width
        )
        picked = vector[send_index]
        outgoing = jnp.where(send_live, picked, jnp.zeros_like(picked))
        both = lax.all_to_all(
            jnp.concatenate([outgoing, slot_sums], axis=1),
            "rows",
            split_axis=0,
            concat_axis=0,
            tiled=True,
        )
        arrived = both[:, :slot_width].reshape(slot_total, local_vecs, block_width)
        returned = both[:, slot_width:].reshape(slot_total, -1)
        near_vec = vector[own_cols]
        result = jnp.einsum("ikab,ikvb->iva", near_blocks, near_vec, precision=exact_mode)
        near_terms = jnp.einsum(
            "ikab,iva->ikvb", near_blocks, vector, precision=exact_mode
        ).reshape(block_rows * block_rows, -1)
        result = result + jnp.dot(own_spread, near_terms, precision=exact_mode).reshape(
            vector.shape
        )
        far_vec = arrived[slot_of_ref]
        far_vec = far_vec.reshape(block_rows, -1, local_vecs, block_width)
        result = result + jnp.einsum("ikab,ikvb->iva", far_blocks, far_vec, precision=exact_mode)
        return result + jnp.dot(spread, returned, precision=exact_mode).reshape(vector.shape)

    def wide(per_column):
        return per_column[None, :, None]

    center_value = center[0]
    base_shift = jnp.min(shifts)
    delta_shift = (shifts - base_shift)[:, None]
    start = right_side
    start_image = apply_h(start)
    half_one = start_image - center_value * start
    start_norm, half_norm = lax.psum(
        jnp.stack([column_dot(start, start), column_dot(half_one, half_one)]), "rows"
    )
    alpha_one = start_norm / (half_norm + base_shift * start_norm)
    op_image = apply_h(half_one) - center_value * half_one + base_shift * start
    residual = start - wide(alpha_one) * op_image
    residual_image = apply_h(residual)
    res_norm = lax.psum(column_dot(residual, residual), "rows")
    beta_one = res_norm / start_norm
    direction = residual + wide(beta_one) * start
    half_two = residual_image - center_value * residual + wide(beta_one) * half_one
    energy = lax.psum(
        column_dot(half_two, half_two) + base_shift * column_dot(direction, direction), "rows"
    )
    from_start, from_residual = filter_factors(
        alpha_one, beta_one, res_norm / energy, delta_shift, filter_weights[:, None]
    )
    filtered = wide(from_start) * start + wide(from_residual) * residual
    applied = wide(from_start) * start_image + wide(from_residual) * residual_image
    column_piece = lax.all_gather(filtered, "cols", axis=1, tiled=True)
    correlation = jnp.einsum("iae,ibe->ab", column_piece, filtered, precision=exact_mode)
    projected = jnp.einsum("iae,ibe->ab", column_piece, applied, precision=exact_mode)
    partial_gram = jnp.stack([correlation, projected])
    summed = lax.psum(partial_gram, "rows")
    row_total = peer_count * block_rows * block_width
    return (filtered, summed[0] / row_total, summed[1] / row_total)


def split(value):
    high = value.astype(jnp.bfloat16)
    low = (value - high.astype(jnp.float32)).astype(jnp.bfloat16)
    return high, low


def lane_sum(value):
    return jnp.sum(value, axis=1, keepdims=True)


def row_sum(value):
    return jnp.sum(value, axis=0, keepdims=True)


def filter_kernel(n_rows, n_cols, groups, *refs):
    (
        blocks_hbm,
        cols_hbm,
        vec_hbm,
        center_ref,
        shifts_hbm,
        weights_hbm,
        out_ref,
        gram_ref,
        ritz_ref,
        *scratch,
    ) = refs
    block_rows, vecs, width = out_ref.shape
    per_row = blocks_hbm.shape[1]
    row_blocks, scratch = scratch[:block_rows], scratch[block_rows:]
    (
        cols_vmem,
        vec_ref,
        shifts_vmem,
        weights_vmem,
        high,
        low,
        running,
        index_vmem,
        mask_vmem,
        index_smem,
        mask_smem,
        lists_send,
        lists,
        vec_send,
        vec_recv,
        prod_send,
        prod_recv,
        col_start,
        col_image,
        image_send,
        sums_send,
        sums_recv,
        known_send,
        known_recv,
        early_send,
        early_recv,
        middle_send,
        middle_recv,
        last_send,
        last_recv,
        energy_send,
        energy_recv,
        load_sems,
        small_sems,
        list_sems,
        vec_sems,
        prod_sems,
        col_sems,
        sums_sems,
        early_sems,
        middle_sems,
        last_sems,
        energy_sems,
    ) = scratch
    far = per_row - block_rows
    mine = block_rows * width
    pair = CAP * width
    peers = n_rows - 1
    slots = CAP * peers
    share = vecs // groups
    me = lax.axis_index("rows")
    me_col = lax.axis_index("cols")
    pending = []

    smalls = [
        pltpu.make_async_copy(src, dst, small_sems.at[i])
        for i, (src, dst) in enumerate(
            [
                (cols_hbm, cols_vmem),
                (vec_hbm, vec_ref),
                (shifts_hbm, shifts_vmem),
                (weights_hbm, weights_vmem),
            ]
        )
    ]
    for copy in smalls:
        copy.start()
    loads = [
        pltpu.make_async_copy(blocks_hbm.at[row], row_blocks[row], load_sems.at[row])
        for row in range(block_rows)
    ]
    for copy in loads:
        copy.start()

    barrier = pltpu.get_barrier_semaphore()
    for step in range(1, n_rows):
        pl.semaphore_signal(barrier, inc=1, device_id={"rows": lax.rem(me + step, n_rows)})
    for step in range(1, n_cols):
        pl.semaphore_signal(barrier, inc=1, device_id={"cols": lax.rem(me_col + step, n_cols)})

    def begin(src, dst, send, recv, where):
        copy = pltpu.make_async_remote_copy(
            src_ref=src,
            dst_ref=dst,
            send_sem=send,
            recv_sem=recv,
            device_id=where,
            device_id_type=pl.DeviceIdType.MESH,
        )
        copy.start()
        pending.append(copy)
        return copy

    def to_row(src, dst, sems, step):
        where = {"rows": lax.rem(me + step, n_rows)}
        return begin(src, dst, sems.at[0, step - 1], sems.at[1, peers - step], where)

    def to_col(src, dst, sems, step):
        where = {"cols": lax.rem(me_col + step, n_cols)}
        return begin(src, dst, sems.at[0, step - 1], sems.at[1, n_cols - 1 - step], where)

    def arrive(copies):
        for copy in copies:
            copy.wait_recv()

    def place_blocks():
        columns = cols_vmem[...]
        place = lax.broadcasted_iota(jnp.int32, columns.shape, 1)
        lane = lax.broadcasted_iota(jnp.int32, (block_rows, width), 1)
        own = columns - me * block_rows
        slot = jnp.full(columns.shape, -1, jnp.int32)
        for step in range(1, n_rows):
            inner = columns - lax.rem(me + step, n_rows) * block_rows
            hit = (place >= block_rows) & (inner >= 0) & (inner < block_rows)
            value = inner.astype(jnp.float32)
            first = jnp.where(hit, value, float(block_rows))
            first = jnp.min(jnp.min(first, axis=1, keepdims=True), axis=0, keepdims=True)
            last = jnp.where(hit, value, -1.0)
            last = jnp.max(jnp.max(last, axis=1, keepdims=True), axis=0, keepdims=True)
            upper = (inner == last.astype(jnp.int32)).astype(jnp.int32)
            slot = jnp.where(hit, CAP * (step - 1) + upper, slot)
            lists_send[step - 1, 0:1, :] = jnp.broadcast_to(first, (1, width))
            lists_send[step - 1, 1:2, :] = jnp.broadcast_to(last, (1, width))
        key = slot * per_row + place
        rank = jnp.zeros(columns.shape, jnp.int32)
        follows = jnp.zeros(columns.shape, jnp.int32)
        for k in range(block_rows, per_row):
            rank = rank + (key[:, k : k + 1] < key).astype(jnp.int32)
            same = (slot[:, k : k + 1] == slot) & (place > k)
            follows = follows | same.astype(jnp.int32)
        order = jnp.zeros(lane.shape, jnp.int32)
        keep = jnp.zeros(lane.shape, jnp.int32)
        ends = jnp.full(lane.shape, -1, jnp.int32)
        live = jnp.zeros(lane.shape, jnp.int32)
        for k in range(block_rows):
            order = order + jnp.where(own[:, k : k + 1] == lane, k, 0)
        for k in range(block_rows, per_row):
            here = rank[:, k : k + 1] == lane - block_rows
            order = order + jnp.where(here, k, 0)
            keep = keep + jnp.where(here, follows[:, k : k + 1], 0)
            ends = ends + (slot[:, k : k + 1] <= lane - per_row).astype(jnp.int32)
            live = live | (slot[:, k : k + 1] == lane - per_row).astype(jnp.int32)
        tail = lane >= per_row
        ends = jnp.minimum(jnp.maximum(ends, 0), far - 1)
        index_vmem[...] = jnp.where(tail, ends, jnp.minimum(order, per_row - 1))
        mask_vmem[...] = jnp.where(tail, live, keep).astype(jnp.float32)
        moves = [
            pltpu.make_async_copy(index_vmem, index_smem, small_sems.at[4]),
            pltpu.make_async_copy(mask_vmem, mask_smem, small_sems.at[5]),
        ]
        for move in moves:
            move.start()
        return moves

    smalls[0].wait()
    moves = place_blocks()
    pl.semaphore_wait(barrier, peers + n_cols - 1)
    list_copies = [
        to_row(lists_send.at[step - 1], lists.at[peers - step], list_sems, step)
        for step in range(1, n_rows)
    ]
    for copy in smalls[1:]:
        copy.wait()
    col_start[me_col] = vec_ref[...]
    start_copies = [
        to_col(vec_ref, col_start.at[me_col], col_sems.at[0], step) for step in range(1, n_cols)
    ]
    for move in moves:
        move.wait()

    chunk = running.shape[1]
    for row in range(block_rows):
        loads[row].wait()
        source = row_blocks[row]

        @pl.loop(0, width // chunk)
        def _(part):
            lines = pl.ds(pl.multiple_of(part * chunk, chunk), chunk)
            target = pl.ds(pl.multiple_of(row * width + part * chunk, chunk), chunk)

            def put(spot, value):
                top, bottom = split(value)
                high[spot, target, :] = top
                low[spot, target, :] = bottom

            total = jnp.zeros((chunk, width), jnp.float32)
            for j in range(far):
                block = source[index_smem[row, block_rows + j], lines, :]
                total = total * mask_smem[row, block_rows + j] + block
                running[j] = total
            for spot in range(block_rows):
                put(spot, source[index_smem[row, spot], lines, :])
            for s in range(slots):
                value = running[index_smem[row, per_row + s]] * mask_smem[row, per_row + s]
                put(block_rows + s, value)

    def flat(ref):
        return jnp.concatenate([ref[i] for i in range(block_rows)], axis=1)

    def named(step, slot, row):
        return jnp.broadcast_to(lists[step - 1, slot : slot + 1, :], (share, width)) == float(row)

    def dot(a, b, transposed):
        return lax.dot_general(
            a, b, (((1,), (1 if transposed else 0,)), ((), ())),
            preferred_element_type=jnp.float32,
        )

    def stacked(value):
        top, bottom = split(value)
        return top, jnp.concatenate([top, bottom], axis=0)

    def times(parts, rhs_high, rhs_low, transposed):
        top, both = parts
        wide_part = dot(both, rhs_high, transposed)
        count = top.shape[0]
        return wide_part[:count] + wide_part[count:] + dot(top, rhs_low, transposed)

    def columns(ref, first, count):
        return jnp.concatenate([ref[first + k] for k in range(count)], axis=1)

    def near(parts, transposed):
        return times(
            parts, columns(high, 0, block_rows), columns(low, 0, block_rows), transposed
        )

    def remote(parts, step, transposed):
        first = block_rows + CAP * (step - 1)
        return times(parts, columns(high, first, CAP), columns(low, first, CAP), transposed)

    sub_lane = lax.broadcasted_iota(jnp.int32, (share, width), 1)
    sub_row = lax.broadcasted_iota(jnp.int32, (share, width), 0)

    def as_row(value, first):
        spread = jnp.where(sub_lane == sub_row + first, value, 0.0)
        return row_sum(spread)

    def as_column(row_value, first):
        spread = jnp.where(sub_lane == sub_row + first, row_value, 0.0)
        return lane_sum(spread)

    def send_sums(turn, g, values):
        packed = as_row(values[0], 0)
        for q, value in enumerate(values[1:]):
            packed = packed + as_row(value, (q + 1) * share)
        sums_send[turn, g] = packed
        return [
            to_row(
                sums_send.at[turn, g],
                sums_recv.at[turn, g, peers - step],
                sums_sems.at[turn, g],
                step,
            )
            for step in range(1, n_rows)
        ]

    def total_sums(turn, g, copies, count):
        arrive(copies)
        total = sums_send[turn, g]
        for step in range(1, n_rows):
            total = total + sums_recv[turn, g, step - 1]
        return [as_column(total, q * share) for q in range(count)]

    def send_vectors(turn, g, vector):
        copies = []
        for step in range(1, n_rows):
            for slot in range(CAP):
                picked = jnp.zeros((share, width), jnp.float32)
                for row in range(block_rows):
                    piece = vector[:, row * width : (row + 1) * width]
                    picked = jnp.where(named(step, slot, row), piece, picked)
                vec_send[turn, g, step - 1, :, slot * width : (slot + 1) * width] = picked
            copies.append(
                to_row(
                    vec_send.at[turn, g, step - 1],
                    vec_recv.at[turn, g, peers - step],
                    vec_sems.at[turn, g],
                    step,
                )
            )
        return copies

    def send_products(turn, g, parts):
        copies = []
        for step in range(1, n_rows):
            prod_send[turn, g, step - 1] = remote(parts, step, False)
            copies.append(
                to_row(
                    prod_send.at[turn, g, step - 1],
                    prod_recv.at[turn, g, peers - step],
                    prod_sems.at[turn, g],
                    step,
                )
            )
        return copies

    def collect(turn, g, result, vectors, products):
        for step in range(1, n_rows):
            vectors[peers - step].wait_recv()
            result = result + remote(stacked(vec_recv[turn, g, step - 1]), step, True)
        pieces = [result[:, row * width : (row + 1) * width] for row in range(block_rows)]
        for step in range(1, n_rows):
            products[peers - step].wait_recv()
            for slot in range(CAP):
                back = prod_recv[turn, g, step - 1, :, slot * width : (slot + 1) * width]
                for row in range(block_rows):
                    pieces[row] = pieces[row] + jnp.where(named(step, slot, row), back, 0.0)
        return jnp.concatenate(pieces, axis=1)

    def local(parts):
        return near(parts, False) + near(parts, True)

    every_group = range(groups)
    center = center_ref[0]
    base = jnp.min(shifts_vmem[...], axis=1, keepdims=True)

    def take(g):
        return slice(g * share, (g + 1) * share)

    start = [
        jnp.concatenate([vec_ref[i, take(g), :] for i in range(block_rows)], axis=1)
        for g in every_group
    ]

    parts = [stacked(start[g]) for g in every_group]
    products = [send_products(0, g, parts[g]) for g in every_group]
    arrive(list_copies)
    vectors = [send_vectors(0, g, start[g]) for g in every_group]
    results = [local(parts[g]) for g in every_group]
    arrive(start_copies)

    def gathered(ref):
        return split(jnp.concatenate([flat(ref.at[c]) for c in range(n_cols)], axis=0))

    every_start = gathered(col_start)

    image, half, sum_copies = [], [], []
    next_parts, next_products, next_vectors, next_results = [], [], [], []
    for g in every_group:
        image.append(collect(0, g, results[g], vectors[g], products[g]))
        half.append(image[g] - center * start[g])
        next_vectors.append(send_vectors(1, g, half[g]))
        next_parts.append(stacked(half[g]))
        next_products.append(send_products(1, g, next_parts[g]))
        own = [lane_sum(start[g] * start[g]), lane_sum(half[g] * half[g])]
        sum_copies.append(send_sums(0, g, own))
        next_results.append(local(next_parts[g]))

    def whole(pieces):
        return jnp.concatenate(pieces, axis=0)

    def send_all(src, dst, sems):
        return [
            to_row(src, dst.at[peers - step], sems, step) for step in range(1, n_rows)
        ]

    count = n_cols * vecs
    early = times(stacked(jnp.concatenate([whole(start), whole(image)], axis=0)), *every_start, True)
    early_send[...] = jnp.concatenate([early[:vecs], early[vecs:]], axis=1)
    early_copies = send_all(early_send, early_recv, early_sems)

    second, residual, alpha, start_norm, norm_copies = [], [], [], [], []
    parts, products, vectors, results = [], [], [], []
    for g in every_group:
        applied = collect(1, g, next_results[g], next_vectors[g], next_products[g])
        second.append(applied - center * half[g])
        norm_one, half_norm = total_sums(0, g, sum_copies[g], 2)
        start_norm.append(norm_one)
        alpha.append(norm_one / (half_norm + base * norm_one))
        residual.append(start[g] - alpha[g] * (second[g] + base * start[g]))
        vectors.append(send_vectors(2, g, residual[g]))
        parts.append(stacked(residual[g]))
        products.append(send_products(2, g, parts[g]))
        norm_copies.append(send_sums(1, g, [lane_sum(residual[g] * residual[g])]))
        for row in range(block_rows):
            image_send[row, take(g), :] = second[g][:, row * width : (row + 1) * width]
    col_image[me_col] = image_send[...]
    image_copies = [
        to_col(image_send, col_image.at[me_col], col_sems.at[1], step)
        for step in range(1, n_cols)
    ]
    results = [local(parts[g]) for g in every_group]

    arrive(image_copies)
    every_image = gathered(col_image)
    middle = times(
        stacked(jnp.concatenate([whole(start), whole(image), whole(second)], axis=0)),
        *every_image,
        True,
    )
    half_vecs = vecs // 2
    middle_send[:vecs] = jnp.concatenate([middle[:vecs], middle[vecs : 2 * vecs]], axis=1)
    middle_send[vecs:] = jnp.concatenate(
        [middle[2 * vecs : 2 * vecs + half_vecs], middle[2 * vecs + half_vecs :]], axis=1
    )
    middle_copies = send_all(middle_send, middle_recv, middle_sems)

    final_image, beta, res_norm = [], [], []
    known = None
    for g in every_group:
        final_image.append(collect(2, g, results[g], vectors[g], products[g]))
        (norm_two,) = total_sums(1, g, norm_copies[g], 1)
        res_norm.append(norm_two)
        beta.append(norm_two / start_norm[g])
    spot = me_col * vecs
    energy = None
    for g in every_group:
        direction = residual[g] + beta[g] * start[g]
        half_two = final_image[g] - center * residual[g] + beta[g] * half[g]
        own = lane_sum(half_two * half_two + base * (direction * direction))
        row_value = as_row(own, spot + g * share)
        energy = row_value if energy is None else energy + row_value
    energy_send[...] = energy
    energy_copies = []
    for row_step in range(n_rows):
        for col_step in range(n_cols):
            if row_step == 0 and col_step == 0:
                continue
            number = row_step * n_cols + col_step - 1
            opposite = ((n_rows - row_step) % n_rows) * n_cols + (n_cols - col_step) % n_cols - 1
            energy_copies.append(
                begin(
                    energy_send,
                    energy_recv.at[opposite],
                    energy_sems.at[0, number],
                    energy_sems.at[1, opposite],
                    {
                        "rows": lax.rem(me + row_step, n_rows),
                        "cols": lax.rem(me_col + col_step, n_cols),
                    },
                )
            )
    last = times(stacked(whole(final_image)), *every_image, True)
    last_send[...] = jnp.concatenate([last[:half_vecs], last[half_vecs:]], axis=1)
    last_copies = send_all(last_send, last_recv, last_sems)

    def known_row(values):
        total = None
        for g in every_group:
            row_value = as_row(values[g], spot + g * share)
            total = row_value if total is None else total + row_value
        return total

    known = [known_row(alpha), known_row(beta), known_row(res_norm)]
    known_send[...] = jnp.concatenate(
        known + [jnp.zeros((8 - len(known), width), jnp.float32)], axis=0
    )
    known_copies = [
        to_col(known_send, known_recv.at[step - 1], col_sems.at[2], n_cols - step)
        for step in range(1, n_cols)
    ]

    def summed(own_ref, recv, copies):
        arrive(copies)
        total = own_ref[...]
        for step in range(1, n_rows):
            total = total + recv[step - 1]
        return total

    early_total = summed(early_send, early_recv, early_copies)
    middle_total = summed(middle_send, middle_recv, middle_copies)
    arrive(known_copies)
    shared = known_send[...]
    for step in range(1, n_cols):
        shared = shared + known_recv[step - 1]
    live = lax.broadcasted_iota(jnp.int32, (1, width), 1) < count
    alpha_one, beta_one, norm_two = [
        jnp.where(live, shared[q : q + 1], 1.0) for q in range(3)
    ]
    arrive(energy_copies)
    total_energy = energy_send[...]
    for number in range(n_rows * n_cols - 1):
        total_energy = total_energy + energy_recv[number]
    alpha_two = norm_two / jnp.where(live, total_energy, 1.0)
    from_start = jnp.zeros((1, width), jnp.float32)
    from_residual = from_start
    for m in range(shifts_vmem.shape[1]):
        delta = shifts_vmem[:, m : m + 1] - base
        weight = weights_vmem[:, m : m + 1]
        zeta_one = 1.0 / (1.0 + delta * alpha_one)
        zeta_two = (
            zeta_one
            * alpha_one
            / (
                alpha_two * beta_one * (1.0 - zeta_one)
                + alpha_one * (1.0 + delta * alpha_two)
            )
        )
        from_start = from_start + weight * (
            alpha_one * zeta_one + alpha_two * beta_one * zeta_one * zeta_two
        )
        from_residual = from_residual + weight * (alpha_two * zeta_two)
    on_start = from_start + from_residual * (1.0 - alpha_one * base)
    on_image = -from_residual * alpha_one

    def own_column(row_value):
        return whole([as_column(row_value, spot + g * share) for g in every_group])

    for g in every_group:
        along_start = as_column(from_start, spot + g * share)
        along_residual = as_column(from_residual, spot + g * share)
        filtered = along_start * start[g] + along_residual * residual[g]
        for row in range(block_rows):
            out_ref[row, take(g), :] = filtered[:, row * width : (row + 1) * width]
    start_b, image_b = own_column(on_start), own_column(on_image)
    first_b, residual_b = own_column(from_start), own_column(from_residual)
    start_a, image_a = on_start[:, :count], on_image[:, :count]
    last_total = summed(last_send, last_recv, last_copies)
    squares = jnp.concatenate([middle_total[vecs:, :count], middle_total[vecs:, count:]], axis=0)
    closing = jnp.concatenate([last_total[:, :count], last_total[:, count:]], axis=0)
    scale = 1.0 / (n_rows * mine)
    gram_ref[...] = scale * (
        start_b * start_a * early_total[:, :count]
        + (start_b * image_a + image_b * start_a) * middle_total[:vecs, :count]
        + image_b * image_a * squares
    )
    ritz_ref[...] = scale * (
        start_b * start_a * early_total[:, count:]
        + (first_b * image_a + image_b * start_a) * middle_total[:vecs, count:]
        + residual_b * image_a * closing
    )
    for copy in pending:
        copy.wait_send()


def deliver_kernel(*refs):
    sems = refs[-1]
    half = (len(refs) - 1) // 2
    copies = [
        pltpu.make_async_copy(refs[i], refs[half + i], sems.at[i]) for i in range(half)
    ]
    for copy in copies:
        copy.start()
    for copy in copies:
        copy.wait()


def deliver(arrays):
    return pl.pallas_call(
        deliver_kernel,
        out_shape=[jax.ShapeDtypeStruct(a.shape, a.dtype) for a in arrays],
        in_specs=[pl.BlockSpec(memory_space=pltpu.VMEM)] * len(arrays),
        out_specs=[pl.BlockSpec(memory_space=pltpu.HBM)] * len(arrays),
        scratch_shapes=[pltpu.SemaphoreType.DMA((len(arrays),))],
        compiler_params=pltpu.CompilerParams(vmem_limit_bytes=1 << 20),
    )(*arrays)


def in_hbm(value):
    return pltpu.with_memory_space_constraint(value, pltpu.HBM)


GROUPS = 1


def fused_shards(
    n_rows, n_cols, hblocks, col_index, right_side, center, shifts, filter_weights
):
    block_rows, per_row, width, _ = hblocks.shape
    vecs = right_side.shape[1]
    peers = n_rows - 1
    slots = CAP * peers
    far = per_row - block_rows
    mine = block_rows * width
    columns = n_cols * vecs
    pair = CAP * width
    groups = GROUPS
    share = vecs // groups
    chunk = 32
    vmem = pl.BlockSpec(memory_space=pltpu.VMEM)
    hbm = pl.BlockSpec(memory_space=pltpu.HBM)
    f32 = jnp.float32
    exchange = pltpu.VMEM((3, groups, peers, share, pair), f32)
    packed = pltpu.VMEM((block_rows + slots, mine, width), jnp.bfloat16)
    all_but_me = n_rows * n_cols - 1
    outputs = pl.pallas_call(
        functools.partial(filter_kernel, n_rows, n_cols, groups),
        out_shape=[
            jax.ShapeDtypeStruct(right_side.shape, f32),
            jax.ShapeDtypeStruct((vecs, columns), f32),
            jax.ShapeDtypeStruct((vecs, columns), f32),
        ],
        in_specs=[hbm, hbm, hbm, pl.BlockSpec(memory_space=pltpu.SMEM), hbm, hbm],
        out_specs=[vmem, vmem, vmem],
        scratch_shapes=[pltpu.VMEM((per_row, width, width), f32)] * block_rows
        + [
            pltpu.VMEM(col_index.shape, jnp.int32),
            pltpu.VMEM(right_side.shape, f32),
            pltpu.VMEM((1, shifts.shape[0]), f32),
            pltpu.VMEM((1, shifts.shape[0]), f32),
            packed,
            packed,
            pltpu.VMEM((far, chunk, width), f32),
            pltpu.VMEM((block_rows, width), jnp.int32),
            pltpu.VMEM((block_rows, width), f32),
            pltpu.SMEM((block_rows, width), jnp.int32),
            pltpu.SMEM((block_rows, width), f32),
            pltpu.VMEM((peers, CAP, width), f32),
            pltpu.VMEM((peers, CAP, width), f32),
            exchange,
            exchange,
            exchange,
            exchange,
            pltpu.VMEM((n_cols,) + right_side.shape, f32),
            pltpu.VMEM((n_cols,) + right_side.shape, f32),
            pltpu.VMEM(right_side.shape, f32),
            pltpu.VMEM((2, groups, 1, width), f32),
            pltpu.VMEM((2, groups, peers, 1, width), f32),
            pltpu.VMEM((8, width), f32),
            pltpu.VMEM((n_cols - 1, 8, width), f32),
            pltpu.VMEM((vecs, 2 * columns), f32),
            pltpu.VMEM((peers, vecs, 2 * columns), f32),
            pltpu.VMEM((vecs + vecs // 2, 2 * columns), f32),
            pltpu.VMEM((peers, vecs + vecs // 2, 2 * columns), f32),
            pltpu.VMEM((vecs // 2, 2 * columns), f32),
            pltpu.VMEM((peers, vecs // 2, 2 * columns), f32),
            pltpu.VMEM((1, width), f32),
            pltpu.VMEM((all_but_me, 1, width), f32),
            pltpu.SemaphoreType.DMA((block_rows,)),
            pltpu.SemaphoreType.DMA((6,)),
            pltpu.SemaphoreType.DMA((2, peers)),
            pltpu.SemaphoreType.DMA((3, groups, 2, peers)),
            pltpu.SemaphoreType.DMA((3, groups, 2, peers)),
            pltpu.SemaphoreType.DMA((3, 2, n_cols - 1)),
            pltpu.SemaphoreType.DMA((2, groups, 2, peers)),
            pltpu.SemaphoreType.DMA((2, peers)),
            pltpu.SemaphoreType.DMA((2, peers)),
            pltpu.SemaphoreType.DMA((2, peers)),
            pltpu.SemaphoreType.DMA((2, all_but_me)),
        ],
        compiler_params=pltpu.CompilerParams(
            collective_id=0, has_side_effects=True, vmem_limit_bytes=48 << 20
        ),
    )(
        in_hbm(hblocks),
        in_hbm(col_index),
        in_hbm(right_side),
        center,
        in_hbm(shifts.reshape(1, -1)),
        in_hbm(filter_weights.reshape(1, -1)),
    )
    filtered, gram, ritz = deliver(outputs)
    return filtered, gram.T, ritz.T


def solution(mesh):
    placed = (P("rows", None, None, None), P("rows", None), P("rows", "cols", None), P(), P(), P())
    n_rows, n_cols = mesh.shape["rows"], mesh.shape["cols"]

    def body(hblocks, col_index, right_side, *rest):
        block_rows, per_row, width = hblocks.shape[:3]
        vecs = right_side.shape[1]
        peers = n_rows - 1
        fits = (
            CAP * peers * block_rows <= block_rows * per_row
            and per_row + CAP * peers <= width
            and 2 * n_cols * vecs == width
            and vecs % (8 * GROUPS) == 0
            and vecs % 16 == 0
        )
        if fits:
            return fused_shards(n_rows, n_cols, hblocks, col_index, right_side, *rest)
        return shards(hblocks, col_index, right_side, *rest)

    return jax.shard_map(
        body,
        mesh=mesh,
        in_specs=placed,
        out_specs=(P("rows", "cols", None), P(None, "cols"), P(None, "cols")),
        check_vma=False,
    )
```

time: 60.3 us -> 51.4 us (0.85)
  Pallas kernels: 56.3 us -> 50 us
  local copies, waits for them, and re-layouts: 2.52 us -> 0 us
    pallas_call x2, Pallas kernels: 56.3 us -> 50 us  [the longest x1 49.3 us: fused_shards(): pl.pallas_call(functools.partial(filter_kernel, n_rows, n_cols, groups),...]
    unnamed x11 -> x0, local copies, waits for them, and re-layouts: 2.52 us -> none
where the time goes in v1:
time: 51.4 us; the launch traced here: 51.2 us
  Pallas kernels  50 us (97%)
  between operations  1.29 us (3%)
    pallas_call x1, Pallas kernels, fused_shards(): pl.pallas_call(functools.partial(filter_kernel, n_rows, n_cols, groups),...  49.3 us

profile of v1, /device:TPU:0, one launch (start us, length us, event | category | flops | bytes accessed | tf_op | source)
XLA Modules:
  0.0 51.2 jit_solution(9696581803153608684)
XLA Ops:
  1.3 49.3 %shard_map.85 = (f32[8,16,128]{2,1,0:T(8,128)S(1)}, f32[16,64]{1,0:T(8,128)S(1)}, f32[16,64]{1,0:T(8,128)S(1)}) custom-call(f32[8,24,128,128]{3,2,1,0:T(8,128)} %refs_0_.1, s32[8,24]{1,0:T(8,128)} %refs_1_.1, f32[8,16,128]{2,1,0:T(8,128)} %refs_2_.1, f32[1]{0:T(128)S(6)} %copy.9.refs_3_, f32[1,8]{1,0:T(1,128)} %bitcast.4, f32[1,8]{1,0:T(1,128)} %bitcast.5), custom_call_target="tpu_custom_call" | custom-call | tf_op jit(solution)/shard_map/pallas_call | solution.py:754
  50.6 0.7 %shard_map.86 = (f32[8,16,128]{2,1,0:T(8,128)}, f32[16,64]{1,0:T(8,128)}, f32[16,64]{1,0:T(8,128)}) custom-call(f32[8,16,128]{2,1,0:T(8,128)S(1)} %get-tuple-element.9.refs_0_, f32[16,64]{1,0:T(8,128)S(1)} %get-tuple-element.10.refs_1_, f32[16,64]{1,0:T(8,128)S(1)} %get-tuple-element.11.refs_2_), custom_call_target="tpu_custom_call" | custom-call | tf_op jit(solution)/shard_map/pallas_call | solution.py:717

commit v2 on v1

v2 whole, which is shorter than its diff:
```python
import functools

import jax
import jax.numpy as jnp
from jax import lax
from jax.experimental import pallas as pl
from jax.experimental.pallas import tpu as pltpu
from jax.sharding import PartitionSpec as P

CAP = 2


exact_mode = lax.Precision.HIGHEST


def column_dot(first_arr, second_arr):
    return jnp.sum(first_arr * second_arr, axis=(0, 2))


def ordered_lists(need_mask, slot_width):
    ranks = jnp.cumsum(need_mask, axis=1)
    positions = lax.broadcasted_iota(jnp.int32, need_mask.shape, 1)
    columns_out = []
    for slot in range(slot_width):
        hit = (need_mask > 0) & (ranks == slot + 1)
        columns_out.append(jnp.sum(jnp.where(hit, positions, 0), axis=1))
    lists = jnp.stack(columns_out, axis=1)
    live = jnp.sum(need_mask, axis=1, keepdims=True) > 0
    return jnp.where(live, lists, -1)


def filter_factors(alpha_one, beta_one, alpha_two, delta_shift, weights):
    zeta_one = 1.0 / (1.0 + delta_shift * alpha_one)
    zeta_two = (
        zeta_one
        * alpha_one
        / (alpha_two * beta_one * (1.0 - zeta_one) + alpha_one * (1.0 + delta_shift * alpha_two))
    )
    from_start = jnp.sum(
        weights * (alpha_one * zeta_one + alpha_two * beta_one * zeta_one * zeta_two), axis=0
    )
    from_residual = jnp.sum(weights * (alpha_two * zeta_two), axis=0)
    return from_start, from_residual


def shards(hblocks, col_index, right_side, center, shifts, filter_weights):
    block_rows = hblocks.shape[0]
    block_width = hblocks.shape[2]
    local_vecs = right_side.shape[1]
    pole_count = shifts.shape[0]
    peer_count = lax.axis_size("rows")
    slot_width = CAP
    device_index = lax.axis_index("rows")
    own_cols = col_index[:, :block_rows] - device_index * block_rows
    far_cols = col_index[:, block_rows:].reshape(-1)
    near_blocks = hblocks[:, :block_rows]
    far_blocks = hblocks[:, block_rows:]
    every_key = jnp.arange(peer_count * block_rows, dtype=jnp.int32)
    need_mask = (
        jnp.any(far_cols[:, None] == every_key[None, :], axis=0)
        .astype(jnp.int32)
        .reshape(peer_count, block_rows)
    )
    incoming_mask = lax.all_to_all(need_mask, "rows", split_axis=0, concat_axis=0, tiled=True)
    send_lists = ordered_lists(incoming_mask, slot_width)
    my_lists = ordered_lists(need_mask, slot_width)
    owners = lax.broadcasted_iota(jnp.int32, my_lists.shape, 0)
    slot_keys = jnp.where(my_lists >= 0, owners * block_rows + my_lists, -1).reshape(-1)
    slot_total = slot_keys.shape[0]
    matches = far_cols[:, None] == slot_keys[None, :]
    picker = matches.astype(jnp.float32)
    slot_numbers = lax.broadcasted_iota(jnp.int32, matches.shape, 1)
    slot_of_ref = jnp.sum(jnp.where(matches, slot_numbers, 0), axis=1)
    row_numbers = jnp.arange(block_rows, dtype=jnp.int32)[:, None]
    spread = (send_lists.reshape(-1)[None, :] == row_numbers).astype(jnp.float32)
    own_spread = (own_cols.reshape(-1)[None, :] == row_numbers).astype(jnp.float32)
    send_index = jnp.maximum(send_lists, 0)
    send_live = (send_lists >= 0)[:, :, None, None]

    def apply_h(vector):
        far_terms = jnp.einsum("ikab,iva->ikvb", far_blocks, vector, precision=exact_mode).reshape(
            far_cols.shape[0], -1
        )
        slot_sums = jnp.dot(picker.T, far_terms, precision=exact_mode).reshape(
            peer_count, slot_width, local_vecs, block_width
        )
        picked = vector[send_index]
        outgoing = jnp.where(send_live, picked, jnp.zeros_like(picked))
        both = lax.all_to_all(
            jnp.concatenate([outgoing, slot_sums], axis=1),
            "rows",
            split_axis=0,
            concat_axis=0,
            tiled=True,
        )
        arrived = both[:, :slot_width].reshape(slot_total, local_vecs, block_width)
        returned = both[:, slot_width:].reshape(slot_total, -1)
        near_vec = vector[own_cols]
        result = jnp.einsum("ikab,ikvb->iva", near_blocks, near_vec, precision=exact_mode)
        near_terms = jnp.einsum(
            "ikab,iva->ikvb", near_blocks, vector, precision=exact_mode
        ).reshape(block_rows * block_rows, -1)
        result = result + jnp.dot(own_spread, near_terms, precision=exact_mode).reshape(
            vector.shape
        )
        far_vec = arrived[slot_of_ref]
        far_vec = far_vec.reshape(block_rows, -1, local_vecs, block_width)
        result = result + jnp.einsum("ikab,ikvb->iva", far_blocks, far_vec, precision=exact_mode)
        return result + jnp.dot(spread, returned, precision=exact_mode).reshape(vector.shape)

    def wide(per_column):
        return per_column[None, :, None]

    center_value = center[0]
    base_shift = jnp.min(shifts)
    delta_shift = (shifts - base_shift)[:, None]
    start = right_side
    start_image = apply_h(start)
    half_one = start_image - center_value * start
    start_norm, half_norm = lax.psum(
        jnp.stack([column_dot(start, start), column_dot(half_one, half_one)]), "rows"
    )
    alpha_one = start_norm / (half_norm + base_shift * start_norm)
    op_image = apply_h(half_one) - center_value * half_one + base_shift * start
    residual = start - wide(alpha_one) * op_image
    residual_image = apply_h(residual)
    res_norm = lax.psum(column_dot(residual, residual), "rows")
    beta_one = res_norm / start_norm
    direction = residual + wide(beta_one) * start
    half_two = residual_image - center_value * residual + wide(beta_one) * half_one
    energy = lax.psum(
        column_dot(half_two, half_two) + base_shift * column_dot(direction, direction), "rows"
    )
    from_start, from_residual = filter_factors(
        alpha_one, beta_one, res_norm / energy, delta_shift, filter_weights[:, None]
    )
    filtered = wide(from_start) * start + wide(from_residual) * residual
    applied = wide(from_start) * start_image + wide(from_residual) * residual_image
    column_piece = lax.all_gather(filtered, "cols", axis=1, tiled=True)
    correlation = jnp.einsum("iae,ibe->ab", column_piece, filtered, precision=exact_mode)
    projected = jnp.einsum("iae,ibe->ab", column_piece, applied, precision=exact_mode)
    partial_gram = jnp.stack([correlation, projected])
    summed = lax.psum(partial_gram, "rows")
    row_total = peer_count * block_rows * block_width
    return (filtered, summed[0] / row_total, summed[1] / row_total)


def split(value):
    high = value.astype(jnp.bfloat16)
    low = (value - high.astype(jnp.float32)).astype(jnp.bfloat16)
    return high, low


def lane_sum(value):
    return jnp.sum(value, axis=1, keepdims=True)


def row_sum(value):
    return jnp.sum(value, axis=0, keepdims=True)


HALF_GAP = 32
SPOT_GAP = 16


def filter_kernel(n_rows, n_cols, refs, accumulators):
    (
        blocks_hbm,
        cols_hbm,
        vec_hbm,
        center_ref,
        shifts_hbm,
        weights_hbm,
        out_ref,
        gram_ref,
        ritz_ref,
        *scratch,
    ) = refs
    block_rows, vecs, width = out_ref.shape
    per_row = blocks_hbm.shape[1]
    row_blocks, scratch = scratch[:block_rows], scratch[block_rows:]
    (
        cols_vmem,
        vec_ref,
        shifts_vmem,
        weights_vmem,
        high,
        low,
        running,
        index_vmem,
        mask_vmem,
        index_smem,
        mask_smem,
        lists_send,
        lists,
        vec_send,
        vec_recv,
        prod_send,
        prod_recv,
        col_start,
        col_image,
        col_second,
        image_send,
        sums_send,
        sums_recv,
        known_send,
        known_recv,
        early_send,
        early_recv,
        early_half,
        early_other,
        middle_send,
        middle_recv,
        middle_half,
        middle_other,
        square_send,
        square_recv,
        last_send,
        last_recv,
        energy_send,
        energy_recv,
        load_sems,
        small_sems,
        vec_sems,
        send_sems,
        recv_sems,
    ) = scratch
    totals, terms, grams = accumulators
    far = per_row - block_rows
    mine = block_rows * width
    peers = n_rows - 1
    slots = CAP * peers
    near_peers = n_rows // 2
    count = n_cols * vecs
    me = lax.axis_index("rows")
    me_col = lax.axis_index("cols")
    drains = []
    used = [0]

    smalls = [
        pltpu.make_async_copy(src, dst, small_sems.at[i])
        for i, (src, dst) in enumerate(
            [
                (cols_hbm, cols_vmem),
                (vec_hbm, vec_ref),
                (shifts_hbm, shifts_vmem),
                (weights_hbm, weights_vmem),
            ]
        )
    ]
    smalls[0].start()
    loads = [
        pltpu.make_async_copy(blocks_hbm.at[row], row_blocks[row], load_sems.at[row])
        for row in range(block_rows)
    ]
    barrier = pltpu.get_barrier_semaphore()
    for step in range(1, n_rows):
        pl.semaphore_signal(barrier, inc=1, device_id={"rows": lax.rem(me + step, n_rows)})
    for step in range(1, n_cols):
        pl.semaphore_signal(barrier, inc=1, device_id={"cols": lax.rem(me_col + step, n_cols)})

    def begin(src, dst, send, recv, where):
        pltpu.make_async_remote_copy(
            src_ref=src,
            dst_ref=dst,
            send_sem=send,
            recv_sem=recv,
            device_id=where,
            device_id_type=pl.DeviceIdType.MESH,
        ).start()

    def row_at(step):
        return {"rows": lax.rem(me + step, n_rows)}

    def col_at(step):
        return {"cols": lax.rem(me_col + step, n_cols)}

    def bytes_of(ref, sem):
        return pltpu.make_async_copy(ref, ref, sem)

    def group(size):
        number = used[0]
        used[0] += 1
        send, recv = send_sems.at[number], recv_sems.at[number]
        drains.append(bytes_of(size, send))
        return send, recv, bytes_of(size, recv)

    def to_all(source, recv_ref):
        send, recv, landed = group(recv_ref)
        for step in range(1, n_rows):
            begin(source(step), recv_ref.at[peers - step], send, recv, row_at(step))
        return landed

    def to_cols(source, recv_ref):
        send, recv, landed = group(recv_ref)
        for step in range(1, n_cols):
            begin(source, recv_ref.at[n_cols - 1 - step], send, recv, col_at(step))
        return landed

    smalls[0].wait()
    for copy in loads + smalls[1:]:
        copy.start()
    columns = cols_vmem[...]
    place = lax.broadcasted_iota(jnp.int32, columns.shape, 1)
    is_far = place >= block_rows
    inside = []
    for step in range(1, n_rows):
        inner = columns - lax.rem(me + step, n_rows) * block_rows
        hit = is_far & (inner >= 0) & (inner < block_rows)
        value = inner.astype(jnp.float32)
        first = jnp.min(jnp.where(hit, value, float(block_rows)), axis=0, keepdims=True)
        first = jnp.min(first, axis=1, keepdims=True)
        last = jnp.max(jnp.where(hit, value, -1.0), axis=0, keepdims=True)
        last = jnp.max(last, axis=1, keepdims=True)
        lists_send[step - 1, 0:1, :] = jnp.broadcast_to(first, (1, width))
        lists_send[step - 1, 1:2, :] = jnp.broadcast_to(last, (1, width))
        inside.append((hit, inner, last))
    pl.semaphore_wait(barrier, peers + n_cols - 1)
    lists_landed = to_all(lambda step: lists_send.at[step - 1], lists)

    def place_blocks():
        lane = lax.broadcasted_iota(jnp.int32, (block_rows, width), 1)
        own = columns - me * block_rows
        slot = jnp.full(columns.shape, -1, jnp.int32)
        for number, (hit, inner, last) in enumerate(inside):
            upper = (inner == last.astype(jnp.int32)).astype(jnp.int32)
            slot = jnp.where(hit, CAP * number + upper, slot)
        key = slot * per_row + place
        rank = jnp.zeros(columns.shape, jnp.int32)
        follows = jnp.zeros(columns.shape, jnp.int32)
        for k in range(block_rows, per_row):
            rank = rank + (key[:, k : k + 1] < key).astype(jnp.int32)
            same = (slot[:, k : k + 1] == slot) & (place > k)
            follows = follows | same.astype(jnp.int32)
        order = jnp.zeros(lane.shape, jnp.int32)
        keep = jnp.zeros(lane.shape, jnp.int32)
        ends = jnp.full(lane.shape, -1, jnp.int32)
        live = jnp.zeros(lane.shape, jnp.int32)
        for k in range(block_rows):
            order = order + jnp.where(own[:, k : k + 1] == lane, k, 0)
        for k in range(block_rows, per_row):
            here = rank[:, k : k + 1] == lane - block_rows
            order = order + jnp.where(here, k, 0)
            keep = keep + jnp.where(here, follows[:, k : k + 1], 0)
            ends = ends + (slot[:, k : k + 1] <= lane - per_row).astype(jnp.int32)
            live = live | (slot[:, k : k + 1] == lane - per_row).astype(jnp.int32)
        tail = lane >= per_row
        ends = jnp.minimum(jnp.maximum(ends, 0), far - 1)
        index_vmem[...] = jnp.where(tail, ends, jnp.minimum(order, per_row - 1))
        mask_vmem[...] = jnp.where(tail, live, keep).astype(jnp.float32)
        moves = [
            pltpu.make_async_copy(index_vmem, index_smem, small_sems.at[4]),
            pltpu.make_async_copy(mask_vmem, mask_smem, small_sems.at[5]),
        ]
        for move in moves:
            move.start()
        return moves

    moves = place_blocks()
    for move in moves:
        move.wait()

    chunk = running.shape[1]
    half_rows = block_rows // 2
    for row in range(block_rows):
        loads[row].wait()
        source = row_blocks[row]
        base_line = row * width + (HALF_GAP if row >= half_rows else 0)

        @pl.loop(0, width // chunk)
        def _(part):
            lines = pl.ds(pl.multiple_of(part * chunk, chunk), chunk)
            target = pl.ds(pl.multiple_of(base_line + part * chunk, 16), chunk)

            def put(spot, value):
                top, bottom = split(value)
                high[spot, target, :] = top
                low[spot, target, :] = bottom

            total = jnp.zeros((chunk, width), jnp.float32)
            for j in range(far):
                block = source[index_smem[row, block_rows + j], lines, :]
                total = total * mask_smem[row, block_rows + j] + block
                running[j] = total
            for spot in range(block_rows):
                put(spot, source[index_smem[row, spot], lines, :])
            for s in range(slots):
                value = running[index_smem[row, per_row + s]] * mask_smem[row, per_row + s]
                put(block_rows + s, value)

    tile = 2 * width
    tiles = block_rows // 2
    staged = [0, 0]

    def feed(unit, weights, transposed, uses):
        register = staged[unit]
        staged[unit] = 1 - register
        pltpu.matmul_push_rhs(weights, register, unit, transpose=transposed)
        for number, (acc, rows) in enumerate(uses):
            pltpu.matmul_acc_lhs(acc, rows, register if number == 0 else None)

    def block(ref, spot, lines):
        begin_at = lines * tile + (HALF_GAP if lines >= tiles // 2 else 0)
        first = slice(begin_at, begin_at + tile)
        return jnp.concatenate([ref[spot, first, :], ref[spot + 1, first, :]], axis=1)

    def multiply(unit, acc, parts, spot, lines, at, transposed):
        top, bottom = [part[:, at * tile : (at + 1) * tile] for part in parts]
        feed(unit, block(high, spot, lines), transposed, [(acc, top), (acc, bottom)])
        feed(unit, block(low, spot, lines), transposed, [(acc, top)])

    half_tiles = tiles // 2

    def sum_of(n):
        return totals[n // half_tiles][n % half_tiles]

    woven = [n + u * half_tiles for n in range(half_tiles) for u in range(2)]

    def flat(ref):
        return jnp.concatenate([ref[i] for i in range(block_rows)], axis=1)

    def piece(value, row):
        return value[:, row * width : (row + 1) * width]

    def named(step, slot, row):
        return jnp.broadcast_to(lists[step - 1, slot : slot + 1, :], (vecs, width)) == float(row)

    lane_of = lax.broadcasted_iota(jnp.int32, (vecs, width), 1)
    row_of = lax.broadcasted_iota(jnp.int32, (vecs, width), 0)

    def as_row(value, first):
        return row_sum(jnp.where(lane_of == row_of + first, value, 0.0))

    def as_column(row_value, first):
        return lane_sum(jnp.where(lane_of == row_of + first, row_value, 0.0))

    def send_sums(turn, values):
        packed = as_row(values[0], 0)
        for q, value in enumerate(values[1:]):
            packed = packed + as_row(value, (q + 1) * vecs)
        sums_send[turn] = packed
        return to_all(lambda step: sums_send.at[turn], sums_recv.at[turn])

    def total_sums(turn, landed, quantities):
        landed.wait()
        total = sums_send[turn]
        for step in range(1, n_rows):
            total = total + sums_recv[turn, step - 1]
        return [as_column(total, q * vecs) for q in range(quantities)]

    def send_vectors(turn, vector):
        number = used[0]
        used[0] += 1
        send = send_sems.at[number]
        drains.append(bytes_of(vec_send.at[turn], send))
        for step in range(1, n_rows):
            for slot in range(CAP):
                picked = jnp.zeros((vecs, width), jnp.float32)
                for row in range(block_rows):
                    picked = jnp.where(named(step, slot, row), piece(vector, row), picked)
                vec_send[turn, step - 1, :, slot * width : (slot + 1) * width] = picked
            begin(
                vec_send.at[turn, step - 1],
                vec_recv.at[turn, peers - step],
                send,
                vec_sems.at[turn, peers - step],
                row_at(step),
            )

    def send_products(turn, parts):
        send, recv, landed = group(prod_recv.at[turn])

        def launch(ready):
            for step, accs in ready:
                value = functools.reduce(jnp.add, [pltpu.matmul_pop(acc) for acc in accs])
                prod_send[turn, step - 1] = value
                begin(
                    prod_send.at[turn, step - 1],
                    prod_recv.at[turn, peers - step],
                    send,
                    recv,
                    row_at(step),
                )

        ready = []
        for first in range(1, n_rows, 2):
            which = (first // 2) % 2
            even, odd = terms[0][which], terms[1][which]
            spot = block_rows + CAP * (first - 1)
            if first + 1 < n_rows:
                for lines in range(tiles):
                    multiply(0, even, parts, spot, lines, lines, False)
                    multiply(1, odd, parts, spot + CAP, lines, lines, False)
                done = [(first, [even]), (first + 1, [odd])]
            else:
                for lines in range(half_tiles):
                    later = lines + half_tiles
                    multiply(0, even, parts, spot, lines, lines, False)
                    multiply(1, odd, parts, spot, later, later, False)
                done = [(first, [even, odd])]
            launch(ready)
            ready = done
        launch(ready)
        return landed

    def local(parts):
        for at in range(tiles):
            for n in woven:
                line = (at + n // half_tiles * half_tiles) % tiles
                multiply(n // half_tiles, sum_of(n), parts, 2 * n, line, line, False)
        for at in range(tiles):
            for n in woven:
                multiply(n // half_tiles, sum_of(n), parts, 2 * at, n, at, True)

    def take_vectors(turn):
        for step in range(1, n_rows):
            bytes_of(vec_recv.at[turn, step - 1], vec_sems.at[turn, step - 1]).wait()
            parts = split(vec_recv[turn, step - 1])
            spot = block_rows + CAP * (step - 1)
            for n in woven:
                multiply(n // half_tiles, sum_of(n), parts, spot, n, 0, True)
        return [pltpu.matmul_pop(sum_of(n)) for n in range(tiles)]

    def take_products(turn, halves, landed):
        result = jnp.concatenate(halves, axis=1)
        pieces = [piece(result, row) for row in range(block_rows)]
        landed.wait()
        for step in range(1, n_rows):
            for slot in range(CAP):
                back = prod_recv[turn, step - 1, :, slot * width : (slot + 1) * width]
                for row in range(block_rows):
                    pieces[row] = pieces[row] + jnp.where(named(step, slot, row), back, 0.0)
        return jnp.concatenate(pieces, axis=1)

    def gathered(own, recv):
        start_at = me_col
        pieces = []
        for c in range(n_cols):
            total = jnp.where(start_at == c, own, 0.0)
            for step in range(1, n_cols):
                other = flat(recv.at[step - 1])
                total = jnp.where(lax.rem(start_at + step, n_cols) == c, other, total)
            pieces.append(total)
        return split(jnp.concatenate(pieces, axis=0))

    def share_columns(number, value, recv_ref):
        for row in range(block_rows):
            image_send[number, row] = piece(value, row)
        return to_cols(image_send.at[number], recv_ref)

    def against(pieces, every):
        top, bottom = split(jnp.concatenate(pieces, axis=0))
        rows = jnp.concatenate([top, bottom], axis=0)
        weights = [part for parts_of in every for part in parts_of]
        weights += [jnp.zeros_like(weights[0])] * (tile // count - len(weights))
        accs = [grams[u][len(pieces) - 1] for u in range(2)]
        for at in range(mine // tile):
            lines = slice(at * tile, (at + 1) * tile)
            tall = jnp.concatenate([weight[:, lines] for weight in weights], axis=0)
            feed(at % 2, tall, True, [(accs[at % 2], rows[:, lines])])
        both = pltpu.matmul_pop(accs[0]) + pltpu.matmul_pop(accs[1])
        half = top.shape[0]
        results = []
        for number in range(len(every)):
            at = 2 * number * count
            wide_part = both[:half, at : at + count] + both[:half, at + count : at + 2 * count]
            results.append(wide_part + both[half:, at : at + count])
        return results

    half_base = me // near_peers * near_peers

    def to_half(source, recv_ref):
        send, recv, landed = group(recv_ref)
        for step in range(1, near_peers):
            where = {"rows": half_base + lax.rem(me - half_base + step, near_peers)}
            begin(source, recv_ref.at[near_peers - 1 - step], send, recv, where)
        return landed

    def to_mirror(landed, own_ref, recv_ref, half_ref, other_ref):
        landed.wait()
        half_ref[...] = summed(own_ref, recv_ref)
        send, recv, crossed = group(other_ref)
        begin(half_ref, other_ref, send, recv, row_at(near_peers))
        return crossed

    def summed(own_ref, recv):
        total = own_ref[...]
        for number in range(recv.shape[0]):
            total = total + recv[number]
        return total

    for copy in smalls[1:]:
        copy.wait()
    center = center_ref[0]
    base = jnp.min(shifts_vmem[...], axis=1, keepdims=True)
    start = flat(vec_ref)

    lists_landed.wait()
    send_vectors(0, start)
    start_landed = to_cols(vec_ref, col_start)
    parts = split(start)
    products = send_products(0, parts)
    local(parts)
    halves = take_vectors(0)
    image = take_products(0, halves, products)

    half = image - center * start
    send_vectors(1, half)
    sums_landed = send_sums(0, [lane_sum(start * start), lane_sum(half * half)])
    image_landed = share_columns(0, image, col_image)
    parts = split(half)
    products = send_products(1, parts)
    local(parts)
    start_landed.wait()
    every_start = gathered(start, col_start)
    early = against([start, image], [every_start])[0]
    early_send[...] = jnp.concatenate([early[:vecs], early[vecs:]], axis=1)
    early_landed = to_half(early_send, early_recv)
    halves = take_vectors(1)
    start_norm, half_norm = total_sums(0, sums_landed, 2)
    alpha = start_norm / (half_norm + base * start_norm)
    applied = take_products(1, halves, products)

    second = applied - center * half
    residual = start - alpha * (second + base * start)
    send_vectors(2, residual)
    norm_landed = send_sums(1, [lane_sum(residual * residual)])
    second_landed = share_columns(1, second, col_second)
    parts = split(residual)
    products = send_products(2, parts)
    early_crossed = to_mirror(early_landed, early_send, early_recv, early_half, early_other)
    image_landed.wait()
    every_image = gathered(image, col_image)
    middle_send[...] = jnp.concatenate(against([second], [every_start, every_image]), axis=1)
    middle_landed = to_half(middle_send, middle_recv)
    local(parts)
    halves = take_vectors(2)

    half_vecs = vecs // 2

    def folded(value):
        return jnp.concatenate([value[:half_vecs], value[half_vecs:]], axis=1)

    def unfolded(value):
        return jnp.concatenate([value[:, :count], value[:, count:]], axis=0)

    (res_norm,) = total_sums(1, norm_landed, 1)
    beta = res_norm / start_norm
    direction = residual + beta * start
    rest = beta * half - center * residual
    own_base = lane_sum(base * (direction * direction))
    spot = me_col * vecs
    known = [as_row(value, spot) for value in (alpha, beta, res_norm)]
    known_send[...] = jnp.concatenate(
        known + [jnp.zeros((8 - len(known), width), jnp.float32)], axis=0
    )
    known_landed = to_cols(known_send, known_recv)
    final_image = take_products(2, halves, products)

    half_two = final_image + rest
    energy_send[...] = as_row(own_base + lane_sum(half_two * half_two), spot)
    send, recv, energy_landed = group(energy_recv)
    for row_step in range(n_rows - 1, -1, -1):
        for col_step in range(n_cols):
            if row_step == 0 and col_step == 0:
                continue
            opposite = ((n_rows - row_step) % n_rows) * n_cols + (n_cols - col_step) % n_cols - 1
            begin(
                energy_send,
                energy_recv.at[opposite],
                send,
                recv,
                {**row_at(row_step), **col_at(col_step)},
            )
    second_landed.wait()
    every_second = gathered(second, col_second)
    last_send[...] = folded(against([final_image], [every_second])[0])
    last_landed = to_all(lambda step: last_send, last_recv)
    square_send[...] = folded(against([second], [every_second])[0])
    square_landed = to_all(lambda step: square_send, square_recv)
    middle_crossed = to_mirror(middle_landed, middle_send, middle_recv, middle_half, middle_other)

    early_crossed.wait()
    early_total = early_half[...] + early_other[...]
    known_landed.wait()
    shared = summed(known_send, known_recv)
    live = lax.broadcasted_iota(jnp.int32, (1, width), 1) < count
    alpha_one, beta_one, norm_two = [
        jnp.where(live, shared[q : q + 1], 1.0) for q in range(3)
    ]
    poles = []
    for m in range(shifts_vmem.shape[1]):
        delta = shifts_vmem[:, m : m + 1] - base
        weight = weights_vmem[:, m : m + 1]
        zeta_one = 1.0 / (1.0 + delta * alpha_one)
        slope = beta_one * (1.0 - zeta_one) + alpha_one * delta
        poles.append((weight, zeta_one, slope))
    middle_crossed.wait()
    middle_total = middle_half[...] + middle_other[...]
    square_landed.wait()
    squares = unfolded(summed(square_send, square_recv))
    crossed, paired = middle_total[:, :count], middle_total[:, count:]
    plain, rayleigh = early_total[:, :count], early_total[:, count:]

    energy_landed.wait()
    alpha_two = norm_two / jnp.where(live, summed(energy_send, energy_recv), 1.0)
    from_start = jnp.zeros((1, width), jnp.float32)
    from_residual = from_start
    for weight, zeta_one, slope in poles:
        zeta_two = zeta_one * alpha_one / (alpha_one + alpha_two * slope)
        from_start = from_start + weight * (
            alpha_one * zeta_one + alpha_two * beta_one * zeta_one * zeta_two
        )
        from_residual = from_residual + weight * (alpha_two * zeta_two)
    on_start = from_start + from_residual * (1.0 - alpha_one * base)
    on_image = -from_residual * alpha_one

    first_b = as_column(from_start, spot)
    residual_b = as_column(from_residual, spot)
    start_b = first_b + residual_b * (1.0 - alpha * base)
    image_b = -residual_b * alpha
    filtered = first_b * start + residual_b * residual
    for row in range(block_rows):
        out_ref[row] = piece(filtered, row)
    start_a, image_a = on_start[:, :count], on_image[:, :count]
    scale = 1.0 / (n_rows * mine)
    gram_ref[...] = scale * (
        start_b * start_a * plain
        + (start_b * image_a + image_b * start_a) * crossed
        + image_b * image_a * squares
    )
    last_landed.wait()
    closing = unfolded(summed(last_send, last_recv))
    ritz_ref[...] = scale * (
        start_b * start_a * rayleigh
        + (first_b * image_a + image_b * start_a) * paired
        + residual_b * image_a * closing
    )
    for drain in drains:
        drain.wait()


def scoped_kernel(n_rows, n_cols, *refs):
    block_rows, vecs, width = refs[6].shape

    def accumulators(rows):
        return [
            [pltpu.ACC(unit)((count, 2 * width), jnp.float32) for count in rows]
            for unit in range(2)
        ]

    pl.run_scoped(
        lambda *accs: filter_kernel(n_rows, n_cols, refs, accs),
        accumulators([vecs] * (block_rows // 4)),
        accumulators([vecs] * 2),
        accumulators([2 * vecs * pieces for pieces in (1, 2)]),
    )


def deliver_kernel(*refs):
    sems = refs[-1]
    half = (len(refs) - 1) // 2
    copies = [
        pltpu.make_async_copy(refs[i], refs[half + i], sems.at[i]) for i in range(half)
    ]
    for copy in copies:
        copy.start()
    for copy in copies:
        copy.wait()


def deliver(arrays):
    return pl.pallas_call(
        deliver_kernel,
        out_shape=[jax.ShapeDtypeStruct(a.shape, a.dtype) for a in arrays],
        in_specs=[pl.BlockSpec(memory_space=pltpu.VMEM)] * len(arrays),
        out_specs=[pl.BlockSpec(memory_space=pltpu.HBM)] * len(arrays),
        scratch_shapes=[pltpu.SemaphoreType.DMA((len(arrays),))],
        compiler_params=pltpu.CompilerParams(vmem_limit_bytes=1 << 20),
    )(*arrays)


def in_hbm(value):
    return pltpu.with_memory_space_constraint(value, pltpu.HBM)


def fused_shards(
    n_rows, n_cols, hblocks, col_index, right_side, center, shifts, filter_weights
):
    block_rows, per_row, width, _ = hblocks.shape
    vecs = right_side.shape[1]
    peers = n_rows - 1
    near_peers = n_rows // 2
    slots = CAP * peers
    far = per_row - block_rows
    mine = block_rows * width
    columns = n_cols * vecs
    pair = CAP * width
    chunk = 32
    vmem = pl.BlockSpec(memory_space=pltpu.VMEM)
    hbm = pl.BlockSpec(memory_space=pltpu.HBM)
    f32 = jnp.float32
    exchange = pltpu.VMEM((3, peers, vecs, pair), f32)
    packed = pltpu.VMEM((block_rows + slots, mine + HALF_GAP + SPOT_GAP, width), jnp.bfloat16)
    gathers = pltpu.VMEM((n_cols - 1,) + right_side.shape, f32)
    product = pltpu.VMEM((vecs, 2 * columns), f32)
    two_stages = [
        product,
        pltpu.VMEM((near_peers - 1, vecs, 2 * columns), f32),
        product,
        product,
    ]
    folded = [
        pltpu.VMEM((vecs // 2, 2 * columns), f32),
        pltpu.VMEM((peers, vecs // 2, 2 * columns), f32),
    ]
    outputs = pl.pallas_call(
        functools.partial(scoped_kernel, n_rows, n_cols),
        out_shape=[
            jax.ShapeDtypeStruct(right_side.shape, f32),
            jax.ShapeDtypeStruct((vecs, columns), f32),
            jax.ShapeDtypeStruct((vecs, columns), f32),
        ],
        in_specs=[hbm, hbm, hbm, pl.BlockSpec(memory_space=pltpu.SMEM), hbm, hbm],
        out_specs=[vmem, vmem, vmem],
        scratch_shapes=[pltpu.VMEM((per_row, width, width), f32)] * block_rows
        + [
            pltpu.VMEM(col_index.shape, jnp.int32),
            pltpu.VMEM(right_side.shape, f32),
            pltpu.VMEM((1, shifts.shape[0]), f32),
            pltpu.VMEM((1, shifts.shape[0]), f32),
            packed,
            packed,
            pltpu.VMEM((far, chunk, width), f32),
            pltpu.VMEM((block_rows, width), jnp.int32),
            pltpu.VMEM((block_rows, width), f32),
            pltpu.SMEM((block_rows, width), jnp.int32),
            pltpu.SMEM((block_rows, width), f32),
            pltpu.VMEM((peers, CAP, width), f32),
            pltpu.VMEM((peers, CAP, width), f32),
            exchange,
            exchange,
            exchange,
            exchange,
            gathers,
            gathers,
            gathers,
            pltpu.VMEM((2,) + right_side.shape, f32),
            pltpu.VMEM((2, 1, width), f32),
            pltpu.VMEM((2, peers, 1, width), f32),
            pltpu.VMEM((8, width), f32),
            pltpu.VMEM((n_cols - 1, 8, width), f32),
            *two_stages,
            *two_stages,
            *folded,
            *folded,
            pltpu.VMEM((1, width), f32),
            pltpu.VMEM((n_rows * n_cols - 1, 1, width), f32),
            pltpu.SemaphoreType.DMA((block_rows,)),
            pltpu.SemaphoreType.DMA((6,)),
            pltpu.SemaphoreType.DMA((3, peers)),
            pltpu.SemaphoreType.DMA((20,)),
            pltpu.SemaphoreType.DMA((20,)),
        ],
        compiler_params=pltpu.CompilerParams(
            collective_id=0, has_side_effects=True, vmem_limit_bytes=48 << 20
        ),
    )(
        in_hbm(hblocks),
        in_hbm(col_index),
        in_hbm(right_side),
        center,
        in_hbm(shifts.reshape(1, -1)),
        in_hbm(filter_weights.reshape(1, -1)),
    )
    filtered, gram, ritz = deliver(outputs)
    return filtered, gram.T, ritz.T


def solution(mesh):
    placed = (P("rows", None, None, None), P("rows", None), P("rows", "cols", None), P(), P(), P())
    n_rows, n_cols = mesh.shape["rows"], mesh.shape["cols"]

    def body(hblocks, col_index, right_side, *rest):
        block_rows, per_row, width = hblocks.shape[:3]
        vecs = right_side.shape[1]
        peers = n_rows - 1
        fits = (
            CAP * peers * block_rows <= block_rows * per_row
            and per_row + CAP * peers <= width
            and 2 * n_cols * vecs == width
            and width == 128
            and block_rows % 4 == 0
            and n_rows % 2 == 0
            and n_rows > 2
            and vecs % 16 == 0
        )
        if fits:
            return fused_shards(n_rows, n_cols, hblocks, col_index, right_side, *rest)
        return shards(hblocks, col_index, right_side, *rest)

    return jax.shard_map(
        body,
        mesh=mesh,
        in_specs=placed,
        out_specs=(P("rows", "cols", None), P(None, "cols"), P(None, "cols")),
        check_vma=False,
    )
```

time: 51.4 us -> 39 us (0.76)
  Pallas kernels: 50 us -> 37.5 us
    pallas_call x1, Pallas kernels: 49.3 us -> 36.9 us  [fused_shards(): pl.pallas_call(functools.partial(scoped_kernel, n_rows, n_cols), out_shap...]
where the time goes in v2:
time: 39 us; the launch traced here: 38.8 us
  Pallas kernels  37.5 us (96%)
  between operations  1.29 us (3%)
    pallas_call x1, Pallas kernels, fused_shards(): pl.pallas_call(functools.partial(scoped_kernel, n_rows, n_cols), out_shap...  36.9 us

profile of v2, /device:TPU:0, one launch (start us, length us, event | category | flops | bytes accessed | tf_op | source)
XLA Modules:
  0.0 38.8 jit_solution(13142201230491786356)
XLA Ops:
  1.3 36.9 %shard_map.85 = (f32[8,16,128]{2,1,0:T(8,128)S(1)}, f32[16,64]{1,0:T(8,128)S(1)}, f32[16,64]{1,0:T(8,128)S(1)}) custom-call(f32[8,24,128,128]{3,2,1,0:T(8,128)} %refs_0_.1, s32[8,24]{1,0:T(8,128)} %refs_1_.1, f32[8,16,128]{2,1,0:T(8,128)} %refs_2_.1, f32[1]{0:T(128)S(6)} %copy.9.refs_3_, f32[1,8]{1,0:T(1,128)} %bitcast.4, f32[1,8]{1,0:T(1,128)} %bitcast.5), custom_call_target="tpu_custom_call" | custom-call | tf_op jit(solution)/shard_map/pallas_call | solution.py:817
  38.2 0.7 %shard_map.86 = (f32[8,16,128]{2,1,0:T(8,128)}, f32[16,64]{1,0:T(8,128)}, f32[16,64]{1,0:T(8,128)}) custom-call(f32[8,16,128]{2,1,0:T(8,128)S(1)} %get-tuple-element.9.refs_0_, f32[16,64]{1,0:T(8,128)S(1)} %get-tuple-element.10.refs_1_, f32[16,64]{1,0:T(8,128)S(1)} %get-tuple-element.11.refs_2_), custom_call_target="tpu_custom_call" | custom-call | tf_op jit(solution)/shard_map/pallas_call | solution.py:773

commit v3 on v2

--- a/solution.py
+++ b/solution.py
@@ -253,6 +253,7 @@
         pltpu.make_async_copy(blocks_hbm.at[row], row_blocks[row], load_sems.at[row])
         for row in range(block_rows)
     ]
+    loads[0].start()
     barrier = pltpu.get_barrier_semaphore()
     for step in range(1, n_rows):
         pl.semaphore_signal(barrier, inc=1, device_id={"rows": lax.rem(me + step, n_rows)})
@@ -272,6 +273,17 @@
     def row_at(step):
         return {"rows": lax.rem(me + step, n_rows)}
 
+    def partner(step):
+        place, bit = me, 1
+        while bit < n_rows:
+            if step & bit:
+                place = place + bit - 2 * bit * lax.rem(lax.div(me, bit), 2)
+            bit *= 2
+        return place
+
+    def mate(step):
+        return {"rows": partner(step)}
+
     def col_at(step):
         return {"cols": lax.rem(me_col + step, n_cols)}
 
@@ -287,8 +299,8 @@
 
     def to_all(source, recv_ref):
         send, recv, landed = group(recv_ref)
-        for step in range(1, n_rows):
-            begin(source(step), recv_ref.at[peers - step], send, recv, row_at(step))
+        for step in range(peers, 0, -1):
+            begin(source(step), recv_ref.at[step - 1], send, recv, mate(step))
         return landed
 
     def to_cols(source, recv_ref):
@@ -298,14 +310,14 @@
         return landed
 
     smalls[0].wait()
-    for copy in loads + smalls[1:]:
+    for copy in loads[1:] + smalls[1:]:
         copy.start()
     columns = cols_vmem[...]
     place = lax.broadcasted_iota(jnp.int32, columns.shape, 1)
     is_far = place >= block_rows
     inside = []
     for step in range(1, n_rows):
-        inner = columns - lax.rem(me + step, n_rows) * block_rows
+        inner = columns - partner(step) * block_rows
         hit = is_far & (inner >= 0) & (inner < block_rows)
         value = inner.astype(jnp.float32)
         first = jnp.min(jnp.where(hit, value, float(block_rows)), axis=0, keepdims=True)
@@ -453,7 +465,7 @@
         used[0] += 1
         send = send_sems.at[number]
         drains.append(bytes_of(vec_send.at[turn], send))
-        for step in range(1, n_rows):
+        for step in range(peers, 0, -1):
             for slot in range(CAP):
                 picked = jnp.zeros((vecs, width), jnp.float32)
                 for row in range(block_rows):
@@ -461,10 +473,10 @@
                 vec_send[turn, step - 1, :, slot * width : (slot + 1) * width] = picked
             begin(
                 vec_send.at[turn, step - 1],
-                vec_recv.at[turn, peers - step],
+                vec_recv.at[turn, step - 1],
                 send,
-                vec_sems.at[turn, peers - step],
-                row_at(step),
+                vec_sems.at[turn, step - 1],
+                mate(step),
             )
 
     def send_products(turn, parts):
@@ -476,14 +488,14 @@
                 prod_send[turn, step - 1] = value
                 begin(
                     prod_send.at[turn, step - 1],
-                    prod_recv.at[turn, peers - step],
+                    prod_recv.at[turn, step - 1],
                     send,
                     recv,
-                    row_at(step),
+                    mate(step),
                 )
 
         ready = []
-        for first in range(1, n_rows, 2):
+        for first in range(peers, 0, -2):
             which = (first // 2) % 2
             even, odd = terms[0][which], terms[1][which]
             spot = block_rows + CAP * (first - 1)
@@ -567,13 +579,10 @@
             results.append(wide_part + both[half:, at : at + count])
         return results
 
-    half_base = me // near_peers * near_peers
-
     def to_half(source, recv_ref):
         send, recv, landed = group(recv_ref)
         for step in range(1, near_peers):
-            where = {"rows": half_base + lax.rem(me - half_base + step, near_peers)}
-            begin(source, recv_ref.at[near_peers - 1 - step], send, recv, where)
+            begin(source, recv_ref.at[step - 1], send, recv, mate(step))
         return landed
 
     def to_mirror(landed, own_ref, recv_ref, half_ref, other_ref):
@@ -680,6 +689,10 @@
     square_landed = to_all(lambda step: square_send, square_recv)
     middle_crossed = to_mirror(middle_landed, middle_send, middle_recv, middle_half, middle_other)
 
+    settled, drains[:] = drains[:], []
+    for drain in settled[:-4]:
+        drain.wait()
+    drains.extend(settled[-4:])
     early_crossed.wait()
     early_total = early_half[...] + early_other[...]
     known_landed.wait()
@@ -891,8 +904,8 @@
             and 2 * n_cols * vecs == width
             and width == 128
             and block_rows % 4 == 0
-            and n_rows % 2 == 0
             and n_rows > 2
+            and n_rows & (n_rows - 1) == 0
             and vecs % 16 == 0
         )
         if fits:

time: 39 us -> 37.4 us (0.959)
  Pallas kernels: 37.5 us -> 35.9 us
    pallas_call x1, Pallas kernels: 36.9 us -> 35.3 us  [fused_shards(): pl.pallas_call(functools.partial(scoped_kernel, n_rows, n_cols), out_shap...]
where the time goes in v3:
time: 37.4 us; the launch traced here: 37.2 us
  Pallas kernels  35.9 us (96%)
  between operations  1.29 us (3%)
    pallas_call x1, Pallas kernels, fused_shards(): pl.pallas_call(functools.partial(scoped_kernel, n_rows, n_cols), out_shap...  35.3 us

profile of v3, /device:TPU:0, one launch (start us, length us, event | category | flops | bytes accessed | tf_op | source)
XLA Modules:
  0.0 37.2 jit_solution(11350933208832134120)
XLA Ops:
  1.3 35.3 %shard_map.85 = (f32[8,16,128]{2,1,0:T(8,128)S(1)}, f32[16,64]{1,0:T(8,128)S(1)}, f32[16,64]{1,0:T(8,128)S(1)}) custom-call(f32[8,24,128,128]{3,2,1,0:T(8,128)} %refs_0_.1, s32[8,24]{1,0:T(8,128)} %refs_1_.1, f32[8,16,128]{2,1,0:T(8,128)} %refs_2_.1, f32[1]{0:T(128)S(6)} %copy.9.refs_3_, f32[1,8]{1,0:T(1,128)} %bitcast.4, f32[1,8]{1,0:T(1,128)} %bitcast.5), custom_call_target="tpu_custom_call" | custom-call | tf_op jit(solution)/shard_map/pallas_call | solution.py:830
  36.6 0.7 %shard_map.86 = (f32[8,16,128]{2,1,0:T(8,128)}, f32[16,64]{1,0:T(8,128)}, f32[16,64]{1,0:T(8,128)}) custom-call(f32[8,16,128]{2,1,0:T(8,128)S(1)} %get-tuple-element.9.refs_0_, f32[16,64]{1,0:T(8,128)S(1)} %get-tuple-element.10.refs_1_, f32[16,64]{1,0:T(8,128)S(1)} %get-tuple-element.11.refs_2_), custom_call_target="tpu_custom_call" | custom-call | tf_op jit(solution)/shard_map/pallas_call | solution.py:786
